TPU v7x, 32 devices: a whole 2x2x4 slice. The times are simulated.
32 devices in a mesh: expert: 8 (over y, x, core), dp: 4 (over z).
Axes of the slice: x: 2, y: 2, z: 4, core: 2. Of those that a mesh axis runs over, the one named last changes fastest.
Arguments:
- tokens: bfloat16 [4096, 2048], P(('expert', 'dp')), may hold values from -6 to 6
- expert_ids: int32 [4096, 8], P(('expert', 'dp')), may hold values from 0 to 15, all different within a row; in each aligned block of 128 rows (0 to 127, 128 to 255, ...) at most 72 rows name the same one
- router: bfloat16 [2048, 16], replicated, may hold values from -0.25 to 0.25
- w_gate: bfloat16 [16, 2048, 640], P('expert'), may hold values from -0.125 to 0.125
- w_up: bfloat16 [16, 2048, 640], P('expert'), may hold values from -0.125 to 0.125
- w_down: bfloat16 [16, 640, 2048], P('expert'), may hold values from -1 to 1
- out_grad: bfloat16 [4096, 2048], P(('expert', 'dp')), may hold values from -6 to 6
Outputs:
- mixed: bfloat16 [4096, 2048], P(('expert', 'dp'))
- token_grad: bfloat16 [4096, 2048], P(('expert', 'dp'))
- router_grad: float32 [2048, 16], replicated
- gate_grad: bfloat16 [16, 2048, 640], P('expert', 'dp')
- up_grad: bfloat16 [16, 2048, 640], P('expert', 'dp')
- down_grad: bfloat16 [16, 640, 2048], P('expert', None, 'dp')
Inputs may be any that keep to these rules, and one draw needn't show every extreme that they name: `expert_ids`: each row names 8 different experts; within the 128 rows of one device no expert is named more than 72 times.
All inputs are finite; a program needn't handle non-finite values.
Results may differ from a plain program's by a relative error of at most 0.008.
Values may be sent and summed in bfloat16 or wider, within the bound.
No kernel may reach another device: no remote copies, remote signals or barrier semaphores. Data moves between devices by JAX's collectives and lax.ppermute only.
A program may use at most 256 MiB of HBM per device.

v0:
```python
import functools

import jax
import jax.numpy as jnp
from jax import lax
from jax.experimental import pallas as pl
from jax.experimental.pallas import tpu as pltpu
from jax.sharding import PartitionSpec as P

F32 = jnp.float32
BF16 = jnp.bfloat16
LANES = 128
PLANE = 8


def mm(a, b, contract):
    return lax.dot_general(a, b, (contract, ((), ())), preferred_element_type=F32)


NN = ((1,), (0,))
NT = ((1,), (1,))
TN = ((0,), (0,))


def expert_kernel(own, last, tok, width, ff, cols, units, *refs):
    refs = list(refs)
    scal = refs.pop(0)
    blocks = [refs.pop(0) for _ in units]
    wc, wd = refs.pop(0), refs.pop(0)
    acc_in = None if own else refs.pop(0)
    outs = [refs.pop(0) for _ in range(3 if last else 1)]
    if own:
        part_outs, rp_out = [refs.pop(0) for _ in range(4)], refs.pop(0)
    x_s, o_s, wc_s, wd_s, pre_s, q_s, gb, acc_s = (refs.pop(0) for _ in range(8))
    if own:
        a_s, sacc = refs.pop(0), refs.pop(0)
    hid, gu = refs.pop(0), refs.pop(0)
    sems = refs.pop(0)
    rows = PLANE * tok
    both = 2 * ff
    chunk_rows = pre_s.shape[0]
    first_expert = scal[0]
    zcol = pl.multiple_of(scal[1] * cols, LANES)
    tiles_e = ff // LANES

    taken = iter(range(64))
    x_copies, o_copies = [], []
    place = 2
    for ref, count in zip(blocks, units):
        for u in range(count):
            at = pl.ds(pl.multiple_of(scal[place] * tok, tok), tok)
            place += 1
            base = 2 * tok * u
            x_copies.append(
                pltpu.make_async_copy(ref.at[pl.ds(base, tok), :], x_s.at[at, :], sems.at[next(taken)])
            )
            o_copies.append(
                pltpu.make_async_copy(
                    ref.at[pl.ds(base + tok, tok), pl.ds(0, width)], o_s.at[at, :], sems.at[next(taken)]
                )
            )

    def part(src, dst, lo, size):
        return pltpu.make_async_copy(
            src.at[:, pl.ds(lo, size)], dst.at[:, pl.ds(lo, size)], sems.at[next(taken)]
        )

    gate_copy = part(wc, wc_s, 0, both)
    up_copy = part(wc, wc_s, both, both + LANES)
    wd_copy = pltpu.make_async_copy(wd, wd_s, sems.at[next(taken)])
    acc_copies = []
    if not own:
        acc_copies = [pltpu.make_async_copy(acc_in, acc_s, sems.at[next(taken)])]
    for copy in [*o_copies, wd_copy, *x_copies, gate_copy, up_copy, *acc_copies]:
        copy.start()
    out_sem = next(taken)
    for copy in [*o_copies, wd_copy]:
        copy.wait()

    def back(c, carry):
        here = pl.ds(pl.multiple_of(c * chunk_rows, chunk_rows), chunk_rows)
        q_s[here, :] = mm(o_s[here, :], wd_s[...], NT)
        return carry

    lax.fori_loop(0, rows // chunk_rows, back, 0)
    for copy in [*x_copies, gate_copy, up_copy]:
        copy.wait()

    lane = lax.broadcasted_iota(jnp.int32, (chunk_rows, LANES), 1)

    def chunk(c, carry):
        here = pl.ds(pl.multiple_of(c * chunk_rows, chunk_rows), chunk_rows)
        pre_s[...] = mm(x_s[here, :width], wc_s[...], NN)
        score = jax.nn.sigmoid(pre_s[:, 2 * both :])
        chosen = score * x_s[here, width:].astype(F32)
        gates = chosen / jnp.sum(chosen, axis=1, keepdims=True)
        for j in range(2):
            col = jnp.sum(jnp.where(lane == first_expert + j, gates, 0.0), axis=1, keepdims=True)
            gb[j, here, :] = jnp.broadcast_to(col, (chunk_rows, LANES))
        if own:
            a_s[here, :] = gates * (1.0 - score)
            sacc[:, here, :] = jnp.zeros((2, chunk_rows, LANES), F32)

        def piece(i, carry):
            r = pl.ds(pl.multiple_of(i * LANES, LANES), LANES)
            ra = pl.ds(pl.multiple_of(c * chunk_rows + i * LANES, LANES), LANES)
            for t in range(both // LANES):
                expert = t // tiles_e
                gate = gb[expert, ra, :]
                pre = pre_s[r, t * LANES : (t + 1) * LANES]
                up = pre_s[r, both + t * LANES : both + (t + 1) * LANES]
                q = q_s[ra, t * LANES : (t + 1) * LANES]
                sig = 0.5 * jnp.tanh(0.5 * pre) + 0.5
                silu = pre * sig
                h = silu * up
                gq = gate * q
                hid[ra, t * LANES : (t + 1) * LANES] = (gate * h).astype(BF16)
                gu[ra, t * LANES : (t + 1) * LANES] = (gq * up * (sig + silu * (1.0 - sig))).astype(BF16)
                gu[ra, both + t * LANES : both + (t + 1) * LANES] = (gq * silu).astype(BF16)
                if own:
                    sacc[expert, ra, :] += h * q
            return carry

        lax.fori_loop(0, chunk_rows // LANES, piece, 0)
        return carry

    lax.fori_loop(0, rows // chunk_rows, chunk, 0)

    for copy in acc_copies:
        copy.wait()
    def weight_grad(i, grad):
        if not own:
            grad = grad + acc_s[i]
        acc_s[i] = grad
        if not last:
            pltpu.make_async_copy(acc_s.at[i], outs[0].at[i], sems.at[out_sem + i]).start()

    def from_tokens(i, carry):
        part = pl.ds(pl.multiple_of(i * both, LANES), both)
        weight_grad(i, mm(x_s[:, pl.ds(zcol, cols)], gu[:, part], TN))
        return carry

    lax.fori_loop(0, 2, from_tokens, 0)
    weight_grad(2, mm(o_s[:, pl.ds(zcol, cols)], hid[...], TN))
    if last:
        for i in range(2):
            for e in range(2):
                outs[i][e] = acc_s[i, :, e * ff : (e + 1) * ff].astype(BF16)
        for e in range(2):
            outs[2][e] = acc_s[2, :, e * ff : (e + 1) * ff].T.astype(BF16)

    if own:
        lane = lax.broadcasted_iota(jnp.int32, (rows, LANES), 1)
        term = jnp.zeros((rows, LANES), F32)
        shared = jnp.zeros((rows, LANES), F32)
        for j in range(2):
            sens = jnp.sum(sacc[j], axis=1, keepdims=True)
            term = term + jnp.where(lane == first_expert + j, sens, 0.0)
            shared = shared + gb[j] * sens
        grad = a_s[...] * (term - shared)
        high = grad.astype(BF16)
        low = (grad - high.astype(F32)).astype(BF16)
        gu[:, 2 * both : 2 * both + LANES] = high
        gu[:, 2 * both + LANES :] = low
        n_out = rp_out.shape[0]
        split = gu[:, 2 * both :]
        terms = mm(split, x_s[:, :width], TN)
        rp_out[...] = terms[:n_out] + terms[LANES : LANES + n_out]

        def mix(c, carry):
            here = pl.ds(pl.multiple_of(c * chunk_rows, chunk_rows), chunk_rows)
            o_s[here, :] = mm(hid[here, :], wd_s[...], NN).astype(BF16)
            return carry

        def token(c, carry):
            here = pl.ds(pl.multiple_of(c * chunk_rows, chunk_rows), chunk_rows)
            grad = mm(gu[here, : 2 * both + LANES], wc_s[...], NT)
            x_s[here, :width] = (grad + mm(gu[here, 2 * both + LANES :], wc_s[:, 2 * both :], NT)).astype(BF16)
            return carry

        finals = []
        for place, (step, kept) in enumerate(((mix, o_s), (token, x_s))):
            lax.fori_loop(0, rows // chunk_rows, step, 0)
            for j in range(2):
                half = pl.ds(j * rows // 2, rows // 2)
                copy = pltpu.make_async_copy(
                    kept.at[half, pl.ds(0, width)], part_outs[2 * place + j], sems.at[out_sem + 3 + 2 * place + j]
                )
                copy.start()
                finals.append(copy)
        for copy in finals:
            copy.wait()
    if not last:
        for i in range(3):
            pltpu.make_async_copy(acc_s.at[i], outs[0].at[i], sems.at[out_sem + i]).wait()


def expert_call(own, last, scal, blocks, wc, wd, acc, n_experts):
    tok = sum(b.shape[0] for b in blocks) // (2 * PLANE)
    units = tuple(b.shape[0] // (2 * tok) for b in blocks)
    both, width = wd.shape
    ff = both // 2
    cols = width // lax.axis_size("dp")
    rows = PLANE * tok
    anywhere = pl.BlockSpec(memory_space=pl.ANY)
    vmem = pl.BlockSpec(memory_space=pltpu.VMEM)
    args = [*blocks, wc, wd]
    if not own:
        args.append(acc)
    if last:
        out_shape = [jax.ShapeDtypeStruct((2, cols, ff), BF16)] * 2 + [jax.ShapeDtypeStruct((2, ff, cols), BF16)]
        out_specs = [vmem] * 3
    else:
        out_shape = [jax.ShapeDtypeStruct((3, cols, both), F32)]
        out_specs = [anywhere]
    if own:
        out_shape += [
            *[jax.ShapeDtypeStruct((rows // 2, width), BF16)] * 4,
            jax.ShapeDtypeStruct((n_experts, width), F32),
        ]
        out_specs += [anywhere] * 4 + [vmem]
    chunk = rows // 4
    scratch = [
        pltpu.VMEM((rows, width + LANES), BF16),
        pltpu.VMEM((rows, width), BF16),
        pltpu.VMEM((width, 2 * both + LANES), BF16),
        pltpu.VMEM((both, width), BF16),
        pltpu.VMEM((chunk, 2 * both + LANES), F32),
        pltpu.VMEM((rows, both), F32),
        pltpu.VMEM((2, rows, LANES), F32),
        pltpu.VMEM((3, cols, both), F32),
    ]
    if own:
        scratch += [pltpu.VMEM((rows, LANES), F32), pltpu.VMEM((2, rows, LANES), F32)]
    scratch += [pltpu.VMEM((rows, both), BF16), pltpu.VMEM((rows, 2 * both + 2 * LANES * own), BF16)]
    scratch.append(pltpu.SemaphoreType.DMA((2 * PLANE + 11,)))
    aliases = {} if own or last else {1 + len(blocks) + 2: 0}
    flops = 2 * rows * width * both * 3 + 2 * rows * cols * both * 3
    return pl.pallas_call(
        functools.partial(expert_kernel, own, last, tok, width, ff, cols, units),
        grid_spec=pltpu.PrefetchScalarGridSpec(
            num_scalar_prefetch=1,
            grid=(),
            in_specs=[anywhere] * len(args),
            out_specs=out_specs,
            scratch_shapes=scratch,
        ),
        out_shape=out_shape,
        input_output_aliases=aliases,
        compiler_params=pltpu.CompilerParams(vmem_limit_bytes=58 * 1024 * 1024),
        cost_estimate=pl.CostEstimate(flops=flops, bytes_accessed=40_000_000, transcendentals=rows * both),
        name="experts_own" if own else "experts_last" if last else "experts_mid",
    )(scal, *args)


def flip(x, even, odd):
    groups = lax.axis_size("expert")
    return lax.ppermute(x, "expert", [(i, i ^ (odd if i % 2 else even)) for i in range(groups)])


def dense_body(tokens, expert_ids, router, w_gate, w_up, w_down, out_grad):
    tok, width = tokens.shape
    n_experts = router.shape[1]
    ff = w_gate.shape[2]
    n_dp = lax.axis_size("dp")
    me = lax.axis_index("expert")
    core = me % 2
    ladder = jnp.arange(LANES, dtype=jnp.int32)
    mask = jnp.any(expert_ids[:, :, None] == ladder[None, None, :], axis=1).astype(BF16)
    block = jnp.concatenate(
        [
            jnp.concatenate([tokens, mask], axis=1),
            jnp.concatenate([out_grad, jnp.zeros((tok, LANES), BF16)], axis=1),
        ],
        axis=0,
    )
    router_pad = jnp.pad(router, ((0, 0), (0, LANES - n_experts)))
    wc = jnp.concatenate([w_gate[0], w_gate[1], w_up[0], w_up[1], router_pad, router_pad], axis=1)
    wd = w_down.reshape(2 * ff, width)
    near_at = jnp.where(core == 0, 1, 2)
    scal = jnp.stack(
        [me * 2, lax.axis_index("dp"), 0, 4, near_at, near_at + 4, 7 - near_at, 3 - near_at, 3, 7]
    ).astype(jnp.int32)
    ring = [(i, (i + 1) % n_dp) for i in range(n_dp)]

    def swap(b):
        return flip(b, 1, 1)

    def pair_of(b):
        return jnp.concatenate([b, swap(b)], axis=0)

    def over_link(b):
        return flip(b, 2, 4)

    def onward(near):
        return flip(near[: 2 * tok], 4, 2)

    def along(b):
        return lax.ppermute(b, "dp", ring)

    def hold(*values):
        return lax.optimization_barrier(values)

    def experts(g, acc, blocks):
        return expert_call(g == 0, g == n_dp - 1, scal, blocks, wc, wd, acc, n_experts)

    def rows_of(x, j):
        return x[j * tok : (j + 1) * tok].astype(F32)

    def core_sums(low, other):
        return [rows_of(low, 0) + rows_of(other, 0)] + [
            (rows_of(low, j) + rows_of(other, j)).astype(BF16) for j in range(1, 4)
        ]

    def plane_total(mine, arrived):
        for a in arrived:
            mine = mine + a.astype(F32)
        return mine.astype(BF16)

    one = along(block)
    pair0 = pair_of(block)
    near0 = over_link(pair0)
    near0, one, wc = hold(near0, one, wc)
    diag0, other0, two, pair1 = onward(near0), swap(near0), along(one), pair_of(one)
    diag0, other0, one, pair1 = hold(diag0, other0, one, pair1)
    blocks0 = [pair0, near0, other0, diag0, swap(diag0)]

    near1, diag1 = over_link(pair1), flip(one, 6, 6)
    acc, mixed_low, mixed_high, token_low, token_high, rp = experts(0, None, blocks0)
    acc, mixed_low, mixed_high, token_low, token_high, rp, near1, diag1, two = hold(
        acc, mixed_low, mixed_high, token_low, token_high, rp, near1, diag1, two
    )
    blocks1 = [pair1, near1, swap(near1), diag1, swap(diag1)]

    pair2 = pair_of(two)
    near2, three = over_link(pair2), along(two)
    rp = rp + swap(rp)
    mixed_other, token_other = swap(mixed_high), swap(token_high)
    (acc,) = experts(1, acc, blocks1)
    acc, near2, three, rp, mixed_other, token_other, mixed_low, token_low = hold(
        acc, near2, three, rp, mixed_other, token_other, mixed_low, token_low
    )

    diag2, other2, pair3 = onward(near2), swap(near2), pair_of(three)
    rp_z = lax.ppermute(rp, "dp", [(i, i ^ 1) for i in range(n_dp)])
    mixed_sums, token_sums = core_sums(mixed_low, mixed_other), core_sums(token_low, token_other)
    acc, diag2, other2, pair3, rp, rp_z, *sums = hold(
        acc, diag2, other2, pair3, rp, rp_z, *mixed_sums, *token_sums
    )
    mixed_sums, token_sums = sums[:4], sums[4:]
    blocks2 = [pair2, near2, other2, diag2, swap(diag2)]

    rp = rp + rp_z
    near3 = over_link(pair3)
    rp_z = lax.ppermute(rp, "dp", [(i, i ^ 2) for i in range(n_dp)])
    mixed_x, mixed_y = flip(mixed_sums[1], 2, 2), flip(mixed_sums[2], 4, 4)
    (acc,) = experts(2, acc, blocks2)
    acc, near3, mixed_x, mixed_y, rp, rp_z = hold(acc, near3, mixed_x, mixed_y, rp, rp_z)

    rp = rp + rp_z
    diag3, other3 = onward(near3), swap(near3)
    rp_x = flip(rp, 2, 2)
    acc, diag3, other3, rp, rp_x, mixed_d, token_3 = hold(
        acc, diag3, other3, rp, rp_x, mixed_sums[3], token_sums[3]
    )
    rp = rp + rp_x
    mixed_d = flip(mixed_d, 6, 6)
    token_parts = [flip(t, k, k) for t, k in zip((*token_sums[1:3], token_3), (2, 4, 6))]
    rp_y = flip(rp, 4, 4)
    out = experts(3, acc, [pair3, near3, other3, diag3, swap(diag3)])
    *out, mixed_d, rp_y, token_x, token_y, token_d = hold(*out, mixed_d, rp_y, *token_parts)
    mixed = plane_total(mixed_sums[0], (mixed_x, mixed_y, mixed_d))
    token_grad = plane_total(token_sums[0], (token_x, token_y, token_d))
    rp = rp + rp_y
    return (mixed, token_grad, rp.T, *out)


def flat_rows(array):
    return array.reshape(array.shape[0], array.shape[1] * array.shape[2], array.shape[3])


def sparse_body(tokens, expert_ids, router, w_gate, w_up, w_down, out_grad):
    f32 = jnp.float32
    bf16 = jnp.bfloat16
    tok_dev, width = tokens.shape
    top = expert_ids.shape[1]
    n_experts = router.shape[1]
    local_experts = w_gate.shape[0]
    groups = lax.axis_size("expert")
    capacity = (tok_dev * top * 9 + 8 * n_experts - 1) // (8 * n_experts)
    n_assign = tok_dev * top
    flat_ids = expert_ids.reshape(-1)
    ladder = jnp.arange(n_experts, dtype=jnp.int32)
    onehot = (flat_ids[:, None] == ladder[None, :]).astype(jnp.int32)
    rank = jnp.sum((jnp.cumsum(onehot, axis=0) - onehot) * onehot, axis=1)
    owner = flat_ids // local_experts
    within = flat_ids % local_experts
    dest = (within * groups + owner) * capacity + rank
    slot_src = jnp.full((n_experts * capacity,), n_assign, jnp.int32)
    slot_src = slot_src.at[dest].set(jnp.arange(n_assign, dtype=jnp.int32))
    live = slot_src < n_assign
    slot_tok = jnp.where(live, slot_src // top, 0)
    logits = jnp.dot(tokens, router, preferred_element_type=f32)
    scores = jax.nn.sigmoid(logits)
    chosen = jnp.take_along_axis(scores, expert_ids, axis=1)
    total = jnp.sum(chosen, axis=1, keepdims=True)
    gates = chosen / total
    gate_slots = jnp.where(live, gates.reshape(-1)[jnp.minimum(slot_src, n_assign - 1)], 0.0)
    send = jnp.where(live[:, None], tokens[slot_tok], jnp.zeros((), bf16))
    send = send.reshape(local_experts, groups, capacity, width)
    piece = lax.all_to_all(send, "expert", split_axis=1, concat_axis=1, tiled=True)
    shape = piece.shape
    rows = flat_rows(piece)
    pre_gate = jnp.einsum("jrd,jdf->jrf", rows, w_gate, preferred_element_type=f32)
    pre_up = jnp.einsum("jrd,jdf->jrf", rows, w_up, preferred_element_type=f32)
    hidden = (pre_gate * jax.nn.sigmoid(pre_gate) * pre_up).astype(bf16)
    expert_out = jnp.einsum("jrf,jfd->jrd", hidden, w_down, preferred_element_type=f32).astype(bf16)
    hid_shape = (shape[0], shape[1], shape[2], hidden.shape[2])
    expert_out = expert_out.reshape(shape)
    hidden = hidden.reshape(hid_shape)
    results = (expert_out, hidden, piece, pre_gate.reshape(hid_shape), pre_up.reshape(hid_shape))
    expert_out = results[0]
    hidden = flat_rows(results[1])
    back = lax.all_to_all(expert_out, "expert", split_axis=1, concat_axis=1, tiled=True).reshape(
        n_experts * capacity, width
    )
    picked = back[dest].reshape(tok_dev, top, width)
    mixed = jnp.einsum("tk,tkd->td", gates, picked.astype(f32)).astype(bf16)
    gate_sens = jnp.einsum("tkd,td->tk", picked, out_grad, preferred_element_type=f32)
    grad_rows = (gate_slots[:, None] * out_grad[slot_tok].astype(f32)).astype(bf16)
    grad_send = jnp.where(live[:, None], grad_rows, jnp.zeros((), bf16))
    grad_send = grad_send.reshape(local_experts, groups, capacity, width)
    grad_in4 = lax.all_to_all(grad_send, "expert", split_axis=1, concat_axis=1, tiled=True)
    grad_in = flat_rows(grad_in4)
    pre_gate = flat_rows(results[3])
    pre_up = flat_rows(results[4])
    hidden_grad = jnp.einsum("jrd,jfd->jrf", grad_in, w_down, preferred_element_type=f32)
    sig = jax.nn.sigmoid(pre_gate)
    silu_val = pre_gate * sig
    gate_term = (hidden_grad * pre_up * sig * (1.0 + pre_gate * (1.0 - sig))).astype(bf16)
    up_term = (hidden_grad * silu_val).astype(bf16)
    input_grad = (
        jnp.einsum("jrf,jdf->jrd", gate_term, w_gate, preferred_element_type=f32)
        + jnp.einsum("jrf,jdf->jrd", up_term, w_up, preferred_element_type=f32)
    ).astype(bf16)
    input_grad = input_grad.reshape(grad_in4.shape)
    returned = lax.all_to_all(
        input_grad, "expert", split_axis=1, concat_axis=1, tiled=True
    ).reshape(n_experts * capacity, width)
    moe_grad = jnp.sum(returned[dest].reshape(tok_dev, top, width).astype(f32), axis=1)
    chosen_grad = (gate_sens - jnp.sum(gate_sens * gates, axis=1, keepdims=True)) / total
    sel_grad = chosen_grad * chosen * (1.0 - chosen)
    pick = (expert_ids[:, :, None] == ladder[None, None, :]).astype(f32)
    logit_grad = jnp.einsum("tk,tke->te", sel_grad, pick).astype(bf16)
    token_grad = (moe_grad + jnp.dot(logit_grad, router.T, preferred_element_type=f32)).astype(bf16)
    router_grad = lax.psum(
        jnp.dot(tokens.T, logit_grad, preferred_element_type=f32), ("expert", "dp")
    )
    hidden_width = hidden.shape[2]
    arrived4 = results[2]
    columns = (
        lax.all_to_all(arrived4, "dp", split_axis=3, concat_axis=1, tiled=True),
        lax.all_to_all(grad_in4, "dp", split_axis=3, concat_axis=1, tiled=True),
    )
    hid_shape = (local_experts, groups, capacity, hidden_width)
    hiddens = (
        lax.all_gather(gate_term.reshape(hid_shape), "dp", axis=1, tiled=True),
        lax.all_gather(up_term.reshape(hid_shape), "dp", axis=1, tiled=True),
        lax.all_gather(results[1], "dp", axis=1, tiled=True),
    )
    x_cols = flat_rows(columns[0])
    g_cols = flat_rows(columns[1])
    gate_grad = jnp.einsum(
        "jrd,jrf->jdf", x_cols, flat_rows(hiddens[0]), preferred_element_type=f32
    ).astype(bf16)
    up_grad = jnp.einsum(
        "jrd,jrf->jdf", x_cols, flat_rows(hiddens[1]), preferred_element_type=f32
    ).astype(bf16)
    down_grad = jnp.einsum(
        "jrf,jrd->jfd", flat_rows(hiddens[2]), g_cols, preferred_element_type=f32
    ).astype(bf16)
    return (mixed, token_grad, router_grad, gate_grad, up_grad, down_grad)


def body(*args):
    plane = lax.axis_size("expert") == 8 and args[3].shape[0] == 2
    line = lax.axis_size("dp")
    return (dense_body if plane and line == 4 else sparse_body)(*args)


def solution(mesh):
    placed = (
        P(("expert", "dp"), None),
        P(("expert", "dp"), None),
        P(),
        P("expert", None, None),
        P("expert", None, None),
        P("expert", None, None),
        P(("expert", "dp"), None),
    )
    return jax.shard_map(
        body,
        mesh=mesh,
        in_specs=placed,
        out_specs=(
            P(("expert", "dp"), None),
            P(("expert", "dp"), None),
            P(),
            P("expert", "dp", None),
            P("expert", "dp", None),
            P("expert", None, "dp"),
        ),
        check_vma=False,
    )
```

profile of v0, /device:TPU:0, one launch (start us, length us, event | category | flops | bytes accessed | tf_op | source)
XLA Modules:
  0.0 284.2 jit_solution(14044600921465179956)
XLA Ops:
  2.9 2.3 pad_maximum_fusion.3
  5.6 2.6 collective-permute-start.2
  8.4 2.9 %collective-permute-start.1 = (bf16[512,2176]{1,0:T(8,128)(2,1)S(1)}, bf16[512,2176]{1,0:T(8,128)(2,1)}, u32[]{:S(2)}, u32[]{:S(2)}) collective-permute-start(bf16[512,2176]{1,0:T(8,128)(2,1)S(1)} %pad_maximum_fusion.refs_1_), channel_id=1, source_target_pairs={{0,8},{4,20},{8,0},{12,28},{16,24},{20,4},{24,16},{28,12},{1,9},{5... | collective-permute-start | bytes 6684680 | tf_op jit(solution)/shard_map/ppermute | solution.py:258
  11.3 1.8 bitcast_dynamic-update-slice_fusion.3
  13.1 1.8 bitcast_dynamic-update-slice_fusion.2
  16.9 3.5 %bitcast_dynamic-update-slice_fusion = bf16[2048,2816]{1,0:T(8,128)(2,1)} fusion(bf16[2048,2816]{1,0:T(8,128)(2,1)} %bitcast_dynamic-update-slice_fusion.1, bf16[2,2048,640]{2,1,0:T(8,128)(2,1)} %param.11), kind=kLoop, calls=%fused_computation | loop fusion | bytes 5242880
  22.3 13.4 %collective-permute-done.2 = bf16[256,2176]{1,0:T(8,128)(2,1)} collective-permute-done((bf16[256,2176]{1,0:T(8,128)(2,1)}, bf16[256,2176]{1,0:T(8,128)(2,1)}, u32[]{:S(2)}, u32[]{:S(2)}) %collective-permute-start.2) | collective-permute-done | bytes 1114144 | tf_op jit(solution)/shard_map/ppermute | solution.py:299
  38.7 2.1 collective-permute-start.3
  40.8 2.2 collective-permute-done.5
  44.4 10.0 %collective-permute-done.3.refs_4_ = bf16[256,2176]{1,0:T(8,128)(2,1)} collective-permute-done((bf16[256,2176]{1,0:T(8,128)(2,1)S(1)}, bf16[256,2176]{1,0:T(8,128)(2,1)}, u32[]{:S(2)}, u32[]{:S(2)}) %collective-permute-start.3) | collective-permute-done | bytes 1114144 | tf_op jit(solution)/shard_map/ppermute | solution.py:258
  55.8 2.0 collective-permute-start.7
  61.6 56.4 %experts_own.1 = (f32[3,512,1280]{2,1,0:T(8,128)}, bf16[512,2048]{1,0:T(8,128)(2,1)}, bf16[512,2048]{1,0:T(8,128)(2,1)}, bf16[512,2048]{1,0:T(8,128)(2,1)}, bf16...) custom-call(s32[10]{0:T(128)} %stack.27.refs_0_, bf16[512,2176]{1,0:T(8,128)(2,1)} %copy-done.2, ...), custom_call_target="tpu_custom_call" | custom-call | flops 20132659200 | bytes 40000000 | tf_op jit(solution)/shard_map/experts_own/pallas_call | solution.py:239
  120.3 5.0 %collective-permute-done.12 = bf16[256,2176]{1,0:T(8,128)(2,1)S(1)} collective-permute-done((bf16[256,2176]{1,0:T(8,128)(2,1)S(1)}, bf16[256,2176]{1,0:T(8,128)(2,1)S(1)}, u32[]{:S(2)}, u32[]{:S(2)}) %collective-permute-start.12) | collective-permute-done | bytes 1114144 | tf_op jit(solution)/shard_map/ppermute | solution.py:258
  128.4 1.9 collective-permute-start.14
  130.3 33.6 %experts_mid.2.refs_8_ = f32[3,512,1280]{2,1,0:T(8,128)} custom-call(s32[10]{0:T(128)} %stack.27.refs_0_, bf16[512,2176]{1,0:T(8,128)(2,1)} %copy-done.1, bf16[512,2176]{1,0:T(8,128)(2,1)} %collective-permute-done.7.refs_2_, bf16[512,2176]{1,0:T(8,128)(2,1)} %collective-permute-done.10.refs_3_, ...), custom_call_target="tpu_custom_call", output_to_operand_aliasing={{}: (8, {})} | custom-call | flops 20132659200 | bytes 40000000 | tf_op jit(solution)/shard_map/experts_mid/pallas_call | solution.py:239
  164.6 2.1 slice.74
  168.8 4.9 %add_convert_fusion.2 = (bf16[128,2048]{1,0:T(8,128)(2,1)S(1)}, bf16[128,2048]{1,0:T(8,128)(2,1)}, bf16[128,2048]{1,0:T(8,128)(2,1)}, f32[128,2048]{1,0:T(8,128)...) fusion(bf16[512,2048]{1,0:T(8,128)(2,1)} %collective-permute-do, ...), kind=kLoop, calls=%fused_computation.10 | loop fusion | flops 7864320 | bytes 13631488 | tf_op jit(solution)/shard_map/convert_element_type | solution.py:312
  175.0 7.2 %collective-permute-done.18.refs_4_ = bf16[256,2176]{1,0:T(8,128)(2,1)S(1)} collective-permute-done((bf16[256,2176]{1,0:T(8,128)(2,1)S(1)}, bf16[256,2176]{1,0:T(8,128)(2,1)S(1)}, u32[]{:S(2)}, u32[]{:S(2)}) %collective-permute-start.18) | collective-permute-done | bytes 1114144 | tf_op jit(solution)/shard_map/ppermute | solution.py:258
  186.7 33.7 %experts_mid.3.refs_8_ = f32[3,512,1280]{2,1,0:T(8,128)} custom-call(s32[10]{0:T(128)} %stack.27.refs_0_, bf16[512,2176]{1,0:T(8,128)(2,1)} %constant_dynamic-update-slice_fusion.refs_1_, bf16[512,2176]{1,0:T(8,128)(2,1)} %collective-permute-done.13.refs_2_, bf16[512,2176]{1,0:T(8,128)(2,1)} %copy-done.11, ...), custom_call_target="tpu_custom_call", output_to_operand_aliasing={{}: (8, {})} | custom-call | flops 20132659200 | bytes 40000000 | tf_op jit(solution)/shard_map/experts_mid/pallas_call | solution.py:239
  224.1 5.8 %collective-permute-done.29 = f32[16,2048]{1,0:T(8,128)S(1)} collective-permute-done((f32[16,2048]{1,0:T(8,128)S(1)}, f32[16,2048]{1,0:T(8,128)S(1)}, u32[]{:S(2)}, u32[]{:S(2)}) %collective-permute-start.29) | collective-permute-done | bytes 131104 | tf_op jit(solution)/shard_map/ppermute | solution.py:258
  229.9 7.9 %collective-permute-done.27.refs_4_ = bf16[256,2176]{1,0:T(8,128)(2,1)S(1)} collective-permute-done((bf16[256,2176]{1,0:T(8,128)(2,1)S(1)}, bf16[256,2176]{1,0:T(8,128)(2,1)S(1)}, u32[]{:S(2)}, u32[]{:S(2)}) %collective-permute-start.27) | collective-permute-done | bytes 1114144 | tf_op jit(solution)/shard_map/ppermute | solution.py:258
  237.8 2.2 collective-permute-start.30
  241.8 1.8 collective-permute-start.31
  246.8 34.1 %experts_last.1 = (bf16[2,512,640]{2,1,0:T(8,128)(2,1)}, bf16[2,512,640]{2,1,0:T(8,128)(2,1)}, bf16[2,640,512]{2,1,0:T(8,128)(2,1)}) custom-call(s32[10]{0:T(128)} %stack.27.refs_0_, bf16[512,2176]{1,0:T(8,128)(2,1)} %copy-done.3, bf16[512,2176]{1,0:T(8,128)(2,1)} %collective-permute-done.23.refs_2_, bf16[512,2176]{1,0:T(8,128)(2,1)} %copy-done.12, ...), custom_call_target="tpu_custom_call" | custom-call | flops 20132659200 | bytes 40000000 | tf_op jit(solution)/shard_map/experts_last/pallas_call | solution.py:239
  (120 shorter events, 41.8 us)
Async XLA Ops:
  5.6 30.1 %collective-permute-start.2 = (bf16[256,2176]{1,0:T(8,128)(2,1)}, bf16[256,2176]{1,0:T(8,128)(2,1)}, u32[]{:S(2)}, u32[]{:S(2)}) collective-permute-start(bf16[256,2176]{1,0:T(8,128)(2,1)} %pad_maximum_fusion.3), channel_id=1, source_target_pairs={{0,1},{1,2},{2,3},{3,0},{4,5},{5,6},{6,7},{7,4},{8,9},{9,10},{10,1... | collective-permute-start | bytes 3342344 | tf_op jit(solution)/shard_map/ppermute | solution.py:299
  8.4 28.4 %collective-permute-start.1 = (bf16[512,2176]{1,0:T(8,128)(2,1)S(1)}, bf16[512,2176]{1,0:T(8,128)(2,1)}, u32[]{:S(2)}, u32[]{:S(2)}) collective-permute-start(bf16[512,2176]{1,0:T(8,128)(2,1)S(1)} %pad_maximum_fusion.refs_1_), channel_id=1, source_target_pairs={{0,8},{4,20},{8,0},{12,28},{16,24},{20,4},{24,16},{28,12},{1,9},{5... | collective-permute-start | bytes 6684680 | tf_op jit(solution)/shard_map/ppermute | solution.py:258
  36.8 17.5 %collective-permute-start.4 = (bf16[512,2176]{1,0:T(8,128)(2,1)}, bf16[512,2176]{1,0:T(8,128)(2,1)S(1)}, u32[]{:S(2)}, u32[]{:S(2)}) collective-permute-start(bf16[512,2176]{1,0:T(8,128)(2,1)} %collective-permute-done.1.refs_2_), channel_id=1, source_target_pairs={{0,4},{4,0},{8,12},{12,8},{16,20},{20,16},{24,28},{28,24},{1,5},{5... | collective-permute-start | bytes 6684680 | tf_op jit(solution)/shard_map/ppermute | solution.py:258
  38.7 15.7 %collective-permute-start.3 = (bf16[256,2176]{1,0:T(8,128)(2,1)S(1)}, bf16[256,2176]{1,0:T(8,128)(2,1)}, u32[]{:S(2)}, u32[]{:S(2)}) collective-permute-start(bf16[256,2176]{1,0:T(8,128)(2,1)S(1)} %slice.73), channel_id=1, source_target_pairs={{0,16},{4,12},{8,24},{12,4},{16,0},{20,28},{24,8},{28,20},{1,17},{... | collective-permute-start | bytes 3342344 | tf_op jit(solution)/shard_map/ppermute | solution.py:258
  55.8 62.3 %collective-permute-start.7 = (bf16[512,2176]{1,0:T(8,128)(2,1)S(1)}, bf16[512,2176]{1,0:T(8,128)(2,1)}, u32[]{:S(2)}, u32[]{:S(2)}) collective-permute-start(bf16[512,2176]{1,0:T(8,128)(2,1)S(1)} %pad_maximum_fusion.1.refs_1_), channel_id=1, source_target_pairs={{0,8},{4,20},{8,0},{12,28},{16,24},{20,4},{24,16},{28,12},{1,9},{5... | collective-permute-start | bytes 6684680 | tf_op jit(solution)/shard_map/ppermute | solution.py:258
  58.4 59.7 %collective-permute-start.9 = (bf16[256,2176]{1,0:T(8,128)(2,1)}, bf16[256,2176]{1,0:T(8,128)(2,1)S(1)}, u32[]{:S(2)}, u32[]{:S(2)}) collective-permute-start(bf16[256,2176]{1,0:T(8,128)(2,1)} %collective-permute-done.2), channel_id=1, source_target_pairs={{0,1},{1,2},{2,3},{3,0},{4,5},{5,6},{6,7},{7,4},{8,9},{9,10},{10,1... | collective-permute-start | bytes 3342344 | tf_op jit(solution)/shard_map/ppermute | solution.py:299
  60.1 57.9 %collective-permute-start.8 = (bf16[256,2176]{1,0:T(8,128)(2,1)}, bf16[256,2176]{1,0:T(8,128)(2,1)}, u32[]{:S(2)}, u32[]{:S(2)}) collective-permute-start(bf16[256,2176]{1,0:T(8,128)(2,1)} %collective-permute-done.2), channel_id=1, source_target_pairs={{0,24},{4,28},{8,16},{12,20},{16,8},{20,12},{24,0},{28,4},{1,25},{... | collective-permute-start | bytes 3342344 | tf_op jit(solution)/shard_map/ppermute | solution.py:258
  126.4 37.6 %collective-permute-start.13 = (bf16[512,2176]{1,0:T(8,128)(2,1)}, bf16[512,2176]{1,0:T(8,128)(2,1)}, u32[]{:S(2)}, u32[]{:S(2)}) collective-permute-start(bf16[512,2176]{1,0:T(8,128)(2,1)} %constant_dynamic-update-slice_fusion.refs_1_), channel_id=1, source_target_pairs={{0,8},{4,20},{8,0},{12,28},{16,24},{20,4},{24,16},{28,12},{1,9},{5... | collective-permute-start | bytes 6684680 | tf_op jit(solution)/shard_map/ppermute | solution.py:258
  127.9 36.1 %collective-permute-start.16 = (bf16[512,2048]{1,0:T(8,128)(2,1)}, bf16[512,2048]{1,0:T(8,128)(2,1)S(1)}, u32[]{:S(2)}, u32[]{:S(2)}) collective-permute-start(bf16[512,2048]{1,0:T(8,128)(2,1)} %get-tuple-element.92), channel_id=1, source_target_pairs={{0,4},{4,0},{8,12},{12,8},{16,20},{20,16},{24,28},{28,24},{1,5},{5... | collective-permute-start | bytes 6291464 | tf_op jit(solution)/shard_map/ppermute | solution.py:258
  127.9 36.1 %collective-permute-start.17 = (bf16[512,2048]{1,0:T(8,128)(2,1)}, bf16[512,2048]{1,0:T(8,128)(2,1)}, u32[]{:S(2)}, u32[]{:S(2)}) collective-permute-start(bf16[512,2048]{1,0:T(8,128)(2,1)} %get-tuple-element.93), channel_id=1, source_target_pairs={{0,4},{4,0},{8,12},{12,8},{16,20},{20,16},{24,28},{28,24},{1,5},{5... | collective-permute-start | bytes 6291464 | tf_op jit(solution)/shard_map/ppermute | solution.py:258
  128.4 35.5 %collective-permute-start.14 = (bf16[256,2176]{1,0:T(8,128)(2,1)S(1)}, bf16[256,2176]{1,0:T(8,128)(2,1)}, u32[]{:S(2)}, u32[]{:S(2)}) collective-permute-start(bf16[256,2176]{1,0:T(8,128)(2,1)S(1)} %collective-permute-done.9), channel_id=1, source_target_pairs={{0,1},{1,2},{2,3},{3,0},{4,5},{5,6},{6,7},{7,4},{8,9},{9,10},{10,1... | collective-permute-start | bytes 3342344 | tf_op jit(solution)/shard_map/ppermute | solution.py:299
  164.0 18.2 %collective-permute-start.19 = (bf16[512,2176]{1,0:T(8,128)(2,1)}, bf16[512,2176]{1,0:T(8,128)(2,1)S(1)}, u32[]{:S(2)}, u32[]{:S(2)}) collective-permute-start(bf16[512,2176]{1,0:T(8,128)(2,1)} %collective-permute-done.13.refs_2_), channel_id=1, source_target_pairs={{0,4},{4,0},{8,12},{12,8},{16,20},{20,16},{24,28},{28,24},{1,5},{5... | collective-permute-start | bytes 6684680 | tf_op jit(solution)/shard_map/ppermute | solution.py:258
  166.6 15.6 %collective-permute-start.18 = (bf16[256,2176]{1,0:T(8,128)(2,1)S(1)}, bf16[256,2176]{1,0:T(8,128)(2,1)S(1)}, u32[]{:S(2)}, u32[]{:S(2)}) collective-permute-start(bf16[256,2176]{1,0:T(8,128)(2,1)S(1)} %slice.74), channel_id=1, source_target_pairs={{0,16},{4,12},{8,24},{12,4},{16,0},{20,28},{24,8},{28,20},{1,17},{... | collective-permute-start | bytes 3342344 | tf_op jit(solution)/shard_map/ppermute | solution.py:258
  182.3 38.6 %collective-permute-start.23 = (bf16[512,2176]{1,0:T(8,128)(2,1)S(1)}, bf16[512,2176]{1,0:T(8,128)(2,1)}, u32[]{:S(2)}, u32[]{:S(2)}) collective-permute-start(bf16[512,2176]{1,0:T(8,128)(2,1)S(1)} %pad_maximum_fusion.2.refs_1_), channel_id=1, source_target_pairs={{0,8},{4,20},{8,0},{12,28},{16,24},{20,4},{24,16},{28,12},{1,9},{5... | collective-permute-start | bytes 6684680 | tf_op jit(solution)/shard_map/ppermute | solution.py:258
  182.9 38.0 %collective-permute-start.24 = (bf16[128,2048]{1,0:T(8,128)(2,1)}, bf16[128,2048]{1,0:T(8,128)(2,1)S(1)}, u32[]{:S(2)}, u32[]{:S(2)}) collective-permute-start(bf16[128,2048]{1,0:T(8,128)(2,1)} %get-tuple-element.109), channel_id=1, source_target_pairs={{0,8},{4,12},{8,0},{12,4},{16,24},{20,28},{24,16},{28,20},{1,9},{5... | collective-permute-start | bytes 1572872 | tf_op jit(solution)/shard_map/ppermute | solution.py:258
  184.4 36.5 %collective-permute-start.25 = (bf16[128,2048]{1,0:T(8,128)(2,1)}, bf16[128,2048]{1,0:T(8,128)(2,1)S(1)}, u32[]{:S(2)}, u32[]{:S(2)}) collective-permute-start(bf16[128,2048]{1,0:T(8,128)(2,1)} %get-tuple-element.110), channel_id=1, source_target_pairs={{0,16},{4,20},{8,24},{12,28},{16,0},{20,4},{24,8},{28,12},{1,17},{... | collective-permute-start | bytes 1572872 | tf_op jit(solution)/shard_map/ppermute | solution.py:258
  184.9 35.4 %collective-permute-start.26 = (f32[16,2048]{1,0:T(8,128)S(1)}, f32[16,2048]{1,0:T(8,128)S(1)}, u32[]{:S(2)}, u32[]{:S(2)}) collective-permute-start(f32[16,2048]{1,0:T(8,128)S(1)} %add.79), channel_id=1, source_target_pairs={{0,2},{1,3},{2,0},{3,1},{4,6},{5,7},{6,4},{7,5},{8,10},{9,11},{10,... | collective-permute-start | bytes 393224 | tf_op jit(solution)/shard_map/ppermute | solution.py:355
  220.9 16.9 %collective-permute-start.28 = (bf16[512,2176]{1,0:T(8,128)(2,1)}, bf16[512,2176]{1,0:T(8,128)(2,1)S(1)}, u32[]{:S(2)}, u32[]{:S(2)}) collective-permute-start(bf16[512,2176]{1,0:T(8,128)(2,1)} %collective-permute-done.23.refs_2_), channel_id=1, source_target_pairs={{0,4},{4,0},{8,12},{12,8},{16,20},{20,16},{24,28},{28,24},{1,5},{5... | collective-permute-start | bytes 6684680 | tf_op jit(solution)/shard_map/ppermute | solution.py:258
  222.3 15.6 %collective-permute-start.27 = (bf16[256,2176]{1,0:T(8,128)(2,1)S(1)}, bf16[256,2176]{1,0:T(8,128)(2,1)S(1)}, u32[]{:S(2)}, u32[]{:S(2)}) collective-permute-start(bf16[256,2176]{1,0:T(8,128)(2,1)S(1)} %slice.91), channel_id=1, source_target_pairs={{0,16},{4,12},{8,24},{12,4},{16,0},{20,28},{24,8},{28,20},{1,17},{... | collective-permute-start | bytes 3342344 | tf_op jit(solution)/shard_map/ppermute | solution.py:258
  240.1 40.8 %collective-permute-start.33 = (bf16[128,2048]{1,0:T(8,128)(2,1)}, bf16[128,2048]{1,0:T(8,128)(2,1)S(1)}, u32[]{:S(2)}, u32[]{:S(2)}) collective-permute-start(bf16[128,2048]{1,0:T(8,128)(2,1)} %get-tuple-element.130), channel_id=1, source_target_pairs={{0,8},{4,12},{8,0},{12,4},{16,24},{20,28},{24,16},{28,20},{1,9},{5... | collective-permute-start | bytes 1572872 | tf_op jit(solution)/shard_map/ppermute | solution.py:258
  240.7 40.1 %collective-permute-start.34 = (bf16[128,2048]{1,0:T(8,128)(2,1)}, bf16[128,2048]{1,0:T(8,128)(2,1)S(1)}, u32[]{:S(2)}, u32[]{:S(2)}) collective-permute-start(bf16[128,2048]{1,0:T(8,128)(2,1)} %get-tuple-element.131), channel_id=1, source_target_pairs={{0,16},{4,20},{8,24},{12,28},{16,0},{20,4},{24,8},{28,12},{1,17},{... | collective-permute-start | bytes 1572872 | tf_op jit(solution)/shard_map/ppermute | solution.py:258
  241.8 39.1 %collective-permute-start.31 = (bf16[128,2048]{1,0:T(8,128)(2,1)}, bf16[128,2048]{1,0:T(8,128)(2,1)S(1)}, u32[]{:S(2)}, u32[]{:S(2)}) collective-permute-start(bf16[128,2048]{1,0:T(8,128)(2,1)} %get-tuple-element.127), channel_id=1, source_target_pairs={{0,24},{4,28},{8,16},{12,20},{16,8},{20,12},{24,0},{28,4},{1,25},{... | collective-permute-start | bytes 1572872 | tf_op jit(solution)/shard_map/ppermute | solution.py:258
  243.6 37.3 %collective-permute-start.32 = (f32[16,2048]{1,0:T(8,128)S(1)}, f32[16,2048]{1,0:T(8,128)S(1)}, u32[]{:S(2)}, u32[]{:S(2)}) collective-permute-start(f32[16,2048]{1,0:T(8,128)S(1)} %add.83), channel_id=1, source_target_pairs={{0,16},{4,20},{8,24},{12,28},{16,0},{20,4},{24,8},{28,12},{1,17},{... | collective-permute-start | bytes 393224 | tf_op jit(solution)/shard_map/ppermute | solution.py:258
  245.7 35.2 %collective-permute-start.35 = (bf16[128,2048]{1,0:T(8,128)(2,1)S(1)}, bf16[128,2048]{1,0:T(8,128)(2,1)S(1)}, u32[]{:S(2)}, u32[]{:S(2)}) collective-permute-start(bf16[128,2048]{1,0:T(8,128)(2,1)S(1)} %get-tuple-element.132), channel_id=1, source_target_pairs={{0,24},{4,28},{8,16},{12,20},{16,8},{20,12},{24,0},{28,4},{1,25},{... | collective-permute-start | bytes 1572872 | tf_op jit(solution)/shard_map/ppermute | solution.py:258
  (31 other events, 325.2 us)
where the time goes:
time: 287 us; the launch traced here: 284 us
  Pallas kernels  158 us (55%)
  waiting for transfers between devices  53.1 us (19%)
  starting transfers between devices  35.6 us (12%)
  local copies, waits for them, and re-layouts  23 us (8%)
  other arithmetic  13.3 us (5%)
    pallas_call x4, Pallas kernels, expert_call(): pl.pallas_call(functools.partial(expert_kernel, own, last, tok, width, ff...  158 us
    ppermute x31, waiting for transfers between devices, flip(): lax.ppermute(x, 'expert', [(i, i ^ (odd if i % 2 else even)) for i in ran...  39.7 us
    ppermute x31, starting transfers between devices, flip(): lax.ppermute(x, 'expert', [(i, i ^ (odd if i % 2 else even)) for i in ran...  26.1 us
    unnamed x46, local copies, waits for them, and re-layouts  14.5 us
    ppermute x3, waiting for transfers between devices, along(): return lax.ppermute(b, 'dp', ring)  13.4 us
    ppermute x3, starting transfers between devices, along(): return lax.ppermute(b, 'dp', ring)  6.19 us
  transfers between devices with their start and end apart: 36, of which 9 were waited for; matrix products, arithmetic and copies ran while one was open for 9% of the time, Pallas kernels for 55%

commit v1 on v0

--- a/solution.py
+++ b/solution.py
@@ -322,53 +322,48 @@
     near0 = over_link(pair0)
     near0, one, wc = hold(near0, one, wc)
     diag0, other0, two, pair1 = onward(near0), swap(near0), along(one), pair_of(one)
-    diag0, other0, one, pair1 = hold(diag0, other0, one, pair1)
+    diag0, other0, one, pair1, two = hold(diag0, other0, one, pair1, two)
     blocks0 = [pair0, near0, other0, diag0, swap(diag0)]
 
-    near1, diag1 = over_link(pair1), flip(one, 6, 6)
+    near1, diag1 = over_link(pair1), along(diag0)
+    three, sibling2 = along(two), swap(two)
     acc, mixed_low, mixed_high, token_low, token_high, rp = experts(0, None, blocks0)
-    acc, mixed_low, mixed_high, token_low, token_high, rp, near1, diag1, two = hold(
-        acc, mixed_low, mixed_high, token_low, token_high, rp, near1, diag1, two
+    acc, mixed_low, mixed_high, token_low, token_high, rp, near1, diag1, three, sibling2 = hold(
+        acc, mixed_low, mixed_high, token_low, token_high, rp, near1, diag1, three, sibling2
     )
     blocks1 = [pair1, near1, swap(near1), diag1, swap(diag1)]
 
-    pair2 = pair_of(two)
-    near2, three = over_link(pair2), along(two)
+    pair2 = jnp.concatenate([two, sibling2], axis=0)
+    near2, diag2 = over_link(pair2), along(diag1)
+    pair3 = pair_of(three)
     rp = rp + swap(rp)
+    rp_z = lax.ppermute(rp, "dp", [(i, i ^ 1) for i in range(n_dp)])
     mixed_other, token_other = swap(mixed_high), swap(token_high)
     (acc,) = experts(1, acc, blocks1)
-    acc, near2, three, rp, mixed_other, token_other, mixed_low, token_low = hold(
-        acc, near2, three, rp, mixed_other, token_other, mixed_low, token_low
-    )
-
-    diag2, other2, pair3 = onward(near2), swap(near2), pair_of(three)
-    rp_z = lax.ppermute(rp, "dp", [(i, i ^ 1) for i in range(n_dp)])
-    mixed_sums, token_sums = core_sums(mixed_low, mixed_other), core_sums(token_low, token_other)
-    acc, diag2, other2, pair3, rp, rp_z, *sums = hold(
-        acc, diag2, other2, pair3, rp, rp_z, *mixed_sums, *token_sums
-    )
-    mixed_sums, token_sums = sums[:4], sums[4:]
-    blocks2 = [pair2, near2, other2, diag2, swap(diag2)]
+    acc, near2, diag2, pair3, rp, rp_z, mixed_other, token_other, mixed_low, token_low = hold(
+        acc, near2, diag2, pair3, rp, rp_z, mixed_other, token_other, mixed_low, token_low
+    )
+    blocks2 = [pair2, near2, swap(near2), diag2, swap(diag2)]
 
     rp = rp + rp_z
-    near3 = over_link(pair3)
     rp_z = lax.ppermute(rp, "dp", [(i, i ^ 2) for i in range(n_dp)])
+    near3, diag3 = over_link(pair3), along(diag2)
+    mixed_sums = core_sums(mixed_low, mixed_other)
     mixed_x, mixed_y = flip(mixed_sums[1], 2, 2), flip(mixed_sums[2], 4, 4)
     (acc,) = experts(2, acc, blocks2)
-    acc, near3, mixed_x, mixed_y, rp, rp_z = hold(acc, near3, mixed_x, mixed_y, rp, rp_z)
+    acc, near3, diag3, mixed_x, mixed_y, rp, rp_z, mixed_d, token_low, token_other = hold(
+        acc, near3, diag3, mixed_x, mixed_y, rp, rp_z, mixed_sums[3], token_low, token_other
+    )
 
     rp = rp + rp_z
-    diag3, other3 = onward(near3), swap(near3)
     rp_x = flip(rp, 2, 2)
-    acc, diag3, other3, rp, rp_x, mixed_d, token_3 = hold(
-        acc, diag3, other3, rp, rp_x, mixed_sums[3], token_sums[3]
-    )
+    token_sums = core_sums(token_low, token_other)
+    mixed_d = flip(mixed_d, 6, 6)
+    token_parts = [flip(t, k, k) for t, k in zip(token_sums[1:], (2, 4, 6))]
+    out = experts(3, acc, [pair3, near3, swap(near3), diag3, swap(diag3)])
+    *out, rp, rp_x, mixed_d, token_x, token_y, token_d = hold(*out, rp, rp_x, mixed_d, *token_parts)
     rp = rp + rp_x
-    mixed_d = flip(mixed_d, 6, 6)
-    token_parts = [flip(t, k, k) for t, k in zip((*token_sums[1:3], token_3), (2, 4, 6))]
     rp_y = flip(rp, 4, 4)
-    out = experts(3, acc, [pair3, near3, other3, diag3, swap(diag3)])
-    *out, mixed_d, rp_y, token_x, token_y, token_d = hold(*out, mixed_d, rp_y, *token_parts)
     mixed = plane_total(mixed_sums[0], (mixed_x, mixed_y, mixed_d))
     token_grad = plane_total(token_sums[0], (token_x, token_y, token_d))
     rp = rp + rp_y

time: 287 us -> 274 us (0.955)
  waiting for transfers between devices: 53.1 us -> 43.7 us
  local copies, waits for them, and re-layouts: 23 us -> 20.1 us
    ppermute x31 -> x28, waiting for transfers between devices: 39.7 us -> 15.8 us  [flip(): lax.ppermute(x, 'expert', [(i, i ^ (odd if i % 2 else even)) for i in ran...]
    ppermute x3 -> x6, waiting for transfers between devices: 13.4 us -> 27.9 us  [along(): return lax.ppermute(b, 'dp', ring)]
    ppermute x31 -> x28, starting transfers between devices: 26.1 us -> 21.3 us  [flip(): lax.ppermute(x, 'expert', [(i, i ^ (odd if i % 2 else even)) for i in ran...]
    slice x3 -> x1, local copies, waits for them, and re-layouts: 4.73 us -> 1.33 us  [onward(): return flip(near[:2 * tok], 4, 2)]
    ppermute x3 -> x6, starting transfers between devices: 6.19 us -> 7.85 us  [along(): return lax.ppermute(b, 'dp', ring)]
    convert_element_type x1 -> x2, other arithmetic: 4.85 us -> 6.28 us  [core_sums(): (rows_of(low, j) + rows_of(other, j)).astype(BF16)]
    unnamed x46 -> x38, local copies, waits for them, and re-layouts: 14.5 us -> 15 us
  transfers between devices with their start and end apart: 36 -> 36, of which waited for: 9 -> 8; matrix products, arithmetic and copies ran while one was open for 9% -> 10% of each run, Pallas kernels for 55% -> 58%
where the time goes in v1:
time: 274 us; the launch traced here: 271 us
  Pallas kernels  158 us (58%)
  waiting for transfers between devices  43.7 us (16%)
  starting transfers between devices  33.2 us (12%)
  local copies, waits for them, and re-layouts  20.1 us (7%)
  other arithmetic  14.6 us (5%)
    pallas_call x4, Pallas kernels, expert_call(): pl.pallas_call(functools.partial(expert_kernel, own, last, tok, width, ff...  158 us
    ppermute x6, waiting for transfers between devices, along(): return lax.ppermute(b, 'dp', ring)  27.9 us
    ppermute x28, starting transfers between devices, flip(): lax.ppermute(x, 'expert', [(i, i ^ (odd if i % 2 else even)) for i in ran...  21.3 us
    ppermute x28, waiting for transfers between devices, flip(): lax.ppermute(x, 'expert', [(i, i ^ (odd if i % 2 else even)) for i in ran...  15.8 us
    unnamed x38, local copies, waits for them, and re-layouts  15 us
    ppermute x6, starting transfers between devices, along(): return lax.ppermute(b, 'dp', ring)  7.85 us
    convert_element_type x2, other arithmetic, core_sums(): (rows_of(low, j) + rows_of(other, j)).astype(BF16)  6.28 us
  transfers between devices with their start and end apart: 36, of which 8 were waited for; matrix products, arithmetic and copies ran while one was open for 10% of the time, Pallas kernels for 58%

profile of v1, /device:TPU:0, one launch (start us, length us, event | category | flops | bytes accessed | tf_op | source)
XLA Modules:
  0.0 270.6 jit_solution(5345843885309505674)
XLA Ops:
  2.9 2.3 pad_maximum_fusion.3
  5.6 2.6 collective-permute-start.2
  8.4 2.9 %collective-permute-start.1 = (bf16[512,2176]{1,0:T(8,128)(2,1)S(1)}, bf16[512,2176]{1,0:T(8,128)(2,1)}, u32[]{:S(2)}, u32[]{:S(2)}) collective-permute-start(bf16[512,2176]{1,0:T(8,128)(2,1)S(1)} %pad_maximum_fusion.refs_1_), channel_id=1, source_target_pairs={{0,8},{4,20},{8,0},{12,28},{16,24},{20,4},{24,16},{28,12},{1,9},{5... | collective-permute-start | bytes 6684680 | tf_op jit(solution)/shard_map/ppermute | solution.py:258
  11.3 1.8 bitcast_dynamic-update-slice_fusion.3
  13.1 1.8 bitcast_dynamic-update-slice_fusion.2
  15.0 1.8 bitcast_dynamic-update-slice_fusion.1
  17.0 3.5 %bitcast_dynamic-update-slice_fusion = bf16[2048,2816]{1,0:T(8,128)(2,1)} fusion(bf16[2048,2816]{1,0:T(8,128)(2,1)} %bitcast_dynamic-update-slice_fusion.1, bf16[2,2048,640]{2,1,0:T(8,128)(2,1)} %param.11), kind=kLoop, calls=%fused_computation | loop fusion | bytes 5242880
  22.5 13.3 %collective-permute-done.2 = bf16[256,2176]{1,0:T(8,128)(2,1)} collective-permute-done((bf16[256,2176]{1,0:T(8,128)(2,1)}, bf16[256,2176]{1,0:T(8,128)(2,1)}, u32[]{:S(2)}, u32[]{:S(2)}) %collective-permute-start.2) | collective-permute-done | bytes 1114144 | tf_op jit(solution)/shard_map/ppermute | solution.py:299
  38.7 2.1 collective-permute-start.3
  44.4 10.0 %collective-permute-done.3.refs_4_ = bf16[256,2176]{1,0:T(8,128)(2,1)} collective-permute-done((bf16[256,2176]{1,0:T(8,128)(2,1)S(1)}, bf16[256,2176]{1,0:T(8,128)(2,1)}, u32[]{:S(2)}, u32[]{:S(2)}) %collective-permute-start.3) | collective-permute-done | bytes 1114144 | tf_op jit(solution)/shard_map/ppermute | solution.py:258
  54.4 14.6 %collective-permute-done.6 = bf16[256,2176]{1,0:T(8,128)(2,1)S(1)} collective-permute-done((bf16[256,2176]{1,0:T(8,128)(2,1)}, bf16[256,2176]{1,0:T(8,128)(2,1)S(1)}, u32[]{:S(2)}, u32[]{:S(2)}) %collective-permute-start.6) | collective-permute-done | bytes 1114144 | tf_op jit(solution)/shard_map/ppermute | solution.py:299
  71.6 1.8 collective-permute-start.10
  74.1 56.4 %experts_own.1 = (f32[3,512,1280]{2,1,0:T(8,128)}, bf16[512,2048]{1,0:T(8,128)(2,1)}, bf16[512,2048]{1,0:T(8,128)(2,1)}, bf16[512,2048]{1,0:T(8,128)(2,1)}, bf16...) custom-call(s32[10]{0:T(128)} %stack.27.refs_0_, bf16[512,2176]{1,0:T(8,128)(2,1)} %copy-done.3, ...), custom_call_target="tpu_custom_call" | custom-call | flops 20132659200 | bytes 40000000 | tf_op jit(solution)/shard_map/experts_own/pallas_call | solution.py:239
  134.7 3.2 %collective-permute-done.17 = f32[16,2048]{1,0:T(8,128)S(1)} collective-permute-done((f32[16,2048]{1,0:T(8,128)S(1)}, f32[16,2048]{1,0:T(8,128)S(1)}, u32[]{:S(2)}, u32[]{:S(2)}) %collective-permute-start.17) | collective-permute-done | bytes 131104 | tf_op jit(solution)/shard_map/ppermute | solution.py:258
  138.7 1.9 collective-permute-start.15
  140.6 2.0 collective-permute-start.18
  142.6 33.4 %experts_mid.2.refs_8_ = f32[3,512,1280]{2,1,0:T(8,128)} custom-call(s32[10]{0:T(128)} %stack.27.refs_0_, bf16[512,2176]{1,0:T(8,128)(2,1)} %copy-done.1, bf16[512,2176]{1,0:T(8,128)(2,1)} %collective-permute-done.8.refs_2_, bf16[512,2176]{1,0:T(8,128)(2,1)} %collective-permute-done.12.refs_3_, ...), custom_call_target="tpu_custom_call", output_to_operand_aliasing={{}: (8, {})} | custom-call | flops 20132659200 | bytes 40000000 | tf_op jit(solution)/shard_map/experts_mid/pallas_call | solution.py:239
  177.9 3.0 %add_convert_fusion.5 = (bf16[128,2048]{1,0:T(8,128)(2,1)S(1)}, bf16[128,2048]{1,0:T(8,128)(2,1)}, bf16[128,2048]{1,0:T(8,128)(2,1)}) fusion(bf16[512,2048]{1,0:T(8,128)(2,1)} %collective-permute-done.19, bf16[512,2048]{1,0:T(8,128)(2,1)S(1)} %copy-done.5), kind=kLoop, calls=%fused_computation.13 | loop fusion | flops 3145728 | bytes 4718592 | tf_op jit(solution)/shard_map/convert_element_type | solution.py:312
  183.2 2.1 collective-permute-start.27
  185.3 33.6 %experts_mid.3.refs_8_ = f32[3,512,1280]{2,1,0:T(8,128)} custom-call(s32[10]{0:T(128)} %stack.27.refs_0_, bf16[512,2176]{1,0:T(8,128)(2,1)} %constant_dynamic-update-slice_fusion.refs_1_, bf16[512,2176]{1,0:T(8,128)(2,1)} %collective-permute-done.14.refs_2_, bf16[512,2176]{1,0:T(8,128)(2,1)} %collective-permute-done.21.refs_3_, ...), custom_call_target="tpu_custom_call", output_to_operand_aliasing={{}: (8, {})} | custom-call | flops 20132659200 | bytes 40000000 | tf_op jit(solution)/shard_map/experts_mid/pallas_call | solution.py:239
  219.6 1.6 collective-permute-start.30
  222.0 3.3 %add_convert_fusion.2 = (bf16[128,2048]{1,0:T(8,128)(2,1)}, bf16[128,2048]{1,0:T(8,128)(2,1)}, bf16[128,2048]{1,0:T(8,128)(2,1)}) fusion(bf16[512,2048]{1,0:T(8,128)(2,1)} %collective-permute-done.20, bf16[512,2048]{1,0:T(8,128)(2,1)} %get-tuple-element.105), kind=kLoop, calls=%fused_computation.10 | loop fusion | flops 3145728 | bytes 4718592 | tf_op jit(solution)/shard_map/convert_element_type | solution.py:312
  230.3 34.3 %experts_last.1 = (bf16[2,512,640]{2,1,0:T(8,128)(2,1)}, bf16[2,512,640]{2,1,0:T(8,128)(2,1)}, bf16[2,640,512]{2,1,0:T(8,128)(2,1)}) custom-call(s32[10]{0:T(128)} %stack.27.refs_0_, bf16[512,2176]{1,0:T(8,128)(2,1)} %copy-done.2, bf16[512,2176]{1,0:T(8,128)(2,1)} %collective-permute-done.23.refs_2_, bf16[512,2176]{1,0:T(8,128)(2,1)} %copy-done.9, ...), custom_call_target="tpu_custom_call" | custom-call | flops 20132659200 | bytes 40000000 | tf_op jit(solution)/shard_map/experts_last/pallas_call | solution.py:239
  265.8 3.3 %add_convert_fusion = (bf16[128,2048]{1,0:T(8,128)(2,1)}, bf16[128,2048]{1,0:T(8,128)(2,1)}) fusion(bf16[128,2048]{1,0:T(8,128)(2,1)S(1)} %collective-permute-done.34, bf16[128,2048]{1,0:T(8,128)(2,1)S(1)} %collective-permute-done.33, bf16[128,2048]{1,0:T(8,128)(2,1)S(1)} %collective-permute-done.32, bf16[512,2048]{1,0:T(8,128)(2,1)} %collective-permute-done.20, ...), kind=kLoop, calls=%fused_computation.8 | loop fusion | flops 5242880 | bytes 6291456 | tf_op jit(solution)/shard_map/convert_element_type | solution.py:318
  (110 shorter events, 32.7 us)
Async XLA Ops:
  5.6 30.1 %collective-permute-start.2 = (bf16[256,2176]{1,0:T(8,128)(2,1)}, bf16[256,2176]{1,0:T(8,128)(2,1)}, u32[]{:S(2)}, u32[]{:S(2)}) collective-permute-start(bf16[256,2176]{1,0:T(8,128)(2,1)} %pad_maximum_fusion.3), channel_id=1, source_target_pairs={{0,1},{1,2},{2,3},{3,0},{4,5},{5,6},{6,7},{7,4},{8,9},{9,10},{10,1... | collective-permute-start | bytes 3342344 | tf_op jit(solution)/shard_map/ppermute | solution.py:299
  8.4 28.4 %collective-permute-start.1 = (bf16[512,2176]{1,0:T(8,128)(2,1)S(1)}, bf16[512,2176]{1,0:T(8,128)(2,1)}, u32[]{:S(2)}, u32[]{:S(2)}) collective-permute-start(bf16[512,2176]{1,0:T(8,128)(2,1)S(1)} %pad_maximum_fusion.refs_1_), channel_id=1, source_target_pairs={{0,8},{4,20},{8,0},{12,28},{16,24},{20,4},{24,16},{28,12},{1,9},{5... | collective-permute-start | bytes 6684680 | tf_op jit(solution)/shard_map/ppermute | solution.py:258
  36.8 32.2 %collective-permute-start.4 = (bf16[512,2176]{1,0:T(8,128)(2,1)}, bf16[512,2176]{1,0:T(8,128)(2,1)S(1)}, u32[]{:S(2)}, u32[]{:S(2)}) collective-permute-start(bf16[512,2176]{1,0:T(8,128)(2,1)} %collective-permute-done.1.refs_2_), channel_id=1, source_target_pairs={{0,4},{4,0},{8,12},{12,8},{16,20},{20,16},{24,28},{28,24},{1,5},{5... | collective-permute-start | bytes 6684680 | tf_op jit(solution)/shard_map/ppermute | solution.py:258
  38.7 15.7 %collective-permute-start.3 = (bf16[256,2176]{1,0:T(8,128)(2,1)S(1)}, bf16[256,2176]{1,0:T(8,128)(2,1)}, u32[]{:S(2)}, u32[]{:S(2)}) collective-permute-start(bf16[256,2176]{1,0:T(8,128)(2,1)S(1)} %slice.67), channel_id=1, source_target_pairs={{0,16},{4,12},{8,24},{12,4},{16,0},{20,28},{24,8},{28,20},{1,17},{... | collective-permute-start | bytes 3342344 | tf_op jit(solution)/shard_map/ppermute | solution.py:258
  40.8 28.2 %collective-permute-start.6 = (bf16[256,2176]{1,0:T(8,128)(2,1)}, bf16[256,2176]{1,0:T(8,128)(2,1)S(1)}, u32[]{:S(2)}, u32[]{:S(2)}) collective-permute-start(bf16[256,2176]{1,0:T(8,128)(2,1)} %collective-permute-done.2), channel_id=1, source_target_pairs={{0,1},{1,2},{2,3},{3,0},{4,5},{5,6},{6,7},{7,4},{8,9},{9,10},{10,1... | collective-permute-start | bytes 3342344 | tf_op jit(solution)/shard_map/ppermute | solution.py:299
  70.4 60.1 %collective-permute-start.8 = (bf16[512,2176]{1,0:T(8,128)(2,1)S(1)}, bf16[512,2176]{1,0:T(8,128)(2,1)}, u32[]{:S(2)}, u32[]{:S(2)}) collective-permute-start(bf16[512,2176]{1,0:T(8,128)(2,1)S(1)} %pad_maximum_fusion.1.refs_1_), channel_id=1, source_target_pairs={{0,8},{4,20},{8,0},{12,28},{16,24},{20,4},{24,16},{28,12},{1,9},{5... | collective-permute-start | bytes 6684680 | tf_op jit(solution)/shard_map/ppermute | solution.py:258
  71.6 58.8 %collective-permute-start.9 = (bf16[256,2176]{1,0:T(8,128)(2,1)}, bf16[256,2176]{1,0:T(8,128)(2,1)}, u32[]{:S(2)}, u32[]{:S(2)}) collective-permute-start(bf16[256,2176]{1,0:T(8,128)(2,1)} %collective-permute-done.3.refs_4_), channel_id=1, source_target_pairs={{0,1},{1,2},{2,3},{3,0},{4,5},{5,6},{6,7},{7,4},{8,9},{9,10},{10,1... | collective-permute-start | bytes 3342344 | tf_op jit(solution)/shard_map/ppermute | solution.py:299
  71.6 58.9 %collective-permute-start.10 = (bf16[256,2176]{1,0:T(8,128)(2,1)S(1)}, bf16[256,2176]{1,0:T(8,128)(2,1)S(1)}, u32[]{:S(2)}, u32[]{:S(2)}) collective-permute-start(bf16[256,2176]{1,0:T(8,128)(2,1)S(1)} %collective-permute-done.6), channel_id=1, source_target_pairs={{0,1},{1,2},{2,3},{3,0},{4,5},{5,6},{6,7},{7,4},{8,9},{9,10},{10,1... | collective-permute-start | bytes 3342344 | tf_op jit(solution)/shard_map/ppermute | solution.py:299
  73.4 57.1 %collective-permute-start.11 = (bf16[256,2176]{1,0:T(8,128)(2,1)S(1)}, bf16[256,2176]{1,0:T(8,128)(2,1)S(1)}, u32[]{:S(2)}, u32[]{:S(2)}) collective-permute-start(bf16[256,2176]{1,0:T(8,128)(2,1)S(1)} %collective-permute-done.6), channel_id=1, source_target_pairs={{0,4},{4,0},{8,12},{12,8},{16,20},{20,16},{24,28},{28,24},{1,5},{5... | collective-permute-start | bytes 3342344 | tf_op jit(solution)/shard_map/ppermute | solution.py:258
  133.8 42.3 %collective-permute-start.14 = (bf16[512,2176]{1,0:T(8,128)(2,1)}, bf16[512,2176]{1,0:T(8,128)(2,1)}, u32[]{:S(2)}, u32[]{:S(2)}) collective-permute-start(bf16[512,2176]{1,0:T(8,128)(2,1)} %constant_dynamic-update-slice_fusion.refs_1_), channel_id=1, source_target_pairs={{0,8},{4,20},{8,0},{12,28},{16,24},{20,4},{24,16},{28,12},{1,9},{5... | collective-permute-start | bytes 6684680 | tf_op jit(solution)/shard_map/ppermute | solution.py:258
  137.9 38.2 %collective-permute-start.19 = (bf16[512,2048]{1,0:T(8,128)(2,1)}, bf16[512,2048]{1,0:T(8,128)(2,1)}, u32[]{:S(2)}, u32[]{:S(2)}) collective-permute-start(bf16[512,2048]{1,0:T(8,128)(2,1)} %get-tuple-element.80), channel_id=1, source_target_pairs={{0,4},{4,0},{8,12},{12,8},{16,20},{20,16},{24,28},{28,24},{1,5},{5... | collective-permute-start | bytes 6291464 | tf_op jit(solution)/shard_map/ppermute | solution.py:258
  138.3 37.8 %collective-permute-start.20 = (bf16[512,2048]{1,0:T(8,128)(2,1)}, bf16[512,2048]{1,0:T(8,128)(2,1)}, u32[]{:S(2)}, u32[]{:S(2)}) collective-permute-start(bf16[512,2048]{1,0:T(8,128)(2,1)} %get-tuple-element.81), channel_id=1, source_target_pairs={{0,4},{4,0},{8,12},{12,8},{16,20},{20,16},{24,28},{28,24},{1,5},{5... | collective-permute-start | bytes 6291464 | tf_op jit(solution)/shard_map/ppermute | solution.py:258
  138.7 37.3 %collective-permute-start.15 = (bf16[256,2176]{1,0:T(8,128)(2,1)}, bf16[256,2176]{1,0:T(8,128)(2,1)}, u32[]{:S(2)}, u32[]{:S(2)}) collective-permute-start(bf16[256,2176]{1,0:T(8,128)(2,1)} %collective-permute-done.9.refs_4_), channel_id=1, source_target_pairs={{0,1},{1,2},{2,3},{3,0},{4,5},{5,6},{6,7},{7,4},{8,9},{9,10},{10,1... | collective-permute-start | bytes 3342344 | tf_op jit(solution)/shard_map/ppermute | solution.py:299
  140.6 35.5 %collective-permute-start.18 = (f32[16,2048]{1,0:T(8,128)S(1)}, f32[16,2048]{1,0:T(8,128)S(1)}, u32[]{:S(2)}, u32[]{:S(2)}) collective-permute-start(f32[16,2048]{1,0:T(8,128)S(1)} %add.70), channel_id=1, source_target_pairs={{0,1},{1,0},{2,3},{3,2},{4,5},{5,4},{6,7},{7,6},{8,9},{9,8},{10,11... | collective-permute-start | bytes 393224 | tf_op jit(solution)/shard_map/ppermute | solution.py:340
  176.7 42.3 %collective-permute-start.24 = (bf16[256,2176]{1,0:T(8,128)(2,1)}, bf16[256,2176]{1,0:T(8,128)(2,1)}, u32[]{:S(2)}, u32[]{:S(2)}) collective-permute-start(bf16[256,2176]{1,0:T(8,128)(2,1)} %collective-permute-done.15.refs_4_), channel_id=1, source_target_pairs={{0,1},{1,2},{2,3},{3,0},{4,5},{5,6},{6,7},{7,4},{8,9},{9,10},{10,1... | collective-permute-start | bytes 3342344 | tf_op jit(solution)/shard_map/ppermute | solution.py:299
  176.7 42.3 %collective-permute-start.23 = (bf16[512,2176]{1,0:T(8,128)(2,1)S(1)}, bf16[512,2176]{1,0:T(8,128)(2,1)}, u32[]{:S(2)}, u32[]{:S(2)}) collective-permute-start(bf16[512,2176]{1,0:T(8,128)(2,1)S(1)} %pad_maximum_fusion.2.refs_1_), channel_id=1, source_target_pairs={{0,8},{4,20},{8,0},{12,28},{16,24},{20,4},{24,16},{28,12},{1,9},{5... | collective-permute-start | bytes 6684680 | tf_op jit(solution)/shard_map/ppermute | solution.py:258
  180.9 38.0 %collective-permute-start.25 = (bf16[128,2048]{1,0:T(8,128)(2,1)}, bf16[128,2048]{1,0:T(8,128)(2,1)S(1)}, u32[]{:S(2)}, u32[]{:S(2)}) collective-permute-start(bf16[128,2048]{1,0:T(8,128)(2,1)} %get-tuple-element.121), channel_id=1, source_target_pairs={{0,8},{4,12},{8,0},{12,4},{16,24},{20,28},{24,16},{28,20},{1,9},{5... | collective-permute-start | bytes 1572872 | tf_op jit(solution)/shard_map/ppermute | solution.py:258
  182.0 37.0 %collective-permute-start.26 = (bf16[128,2048]{1,0:T(8,128)(2,1)}, bf16[128,2048]{1,0:T(8,128)(2,1)S(1)}, u32[]{:S(2)}, u32[]{:S(2)}) collective-permute-start(bf16[128,2048]{1,0:T(8,128)(2,1)} %get-tuple-element.120), channel_id=1, source_target_pairs={{0,16},{4,20},{8,24},{12,28},{16,0},{20,4},{24,8},{28,12},{1,17},{... | collective-permute-start | bytes 1572872 | tf_op jit(solution)/shard_map/ppermute | solution.py:258
  183.2 35.7 %collective-permute-start.27 = (f32[16,2048]{1,0:T(8,128)S(1)}, f32[16,2048]{1,0:T(8,128)S(1)}, u32[]{:S(2)}, u32[]{:S(2)}) collective-permute-start(f32[16,2048]{1,0:T(8,128)S(1)} %add.74), channel_id=1, source_target_pairs={{0,2},{1,3},{2,0},{3,1},{4,6},{5,7},{6,4},{7,5},{8,10},{9,11},{10,... | collective-permute-start | bytes 393224 | tf_op jit(solution)/shard_map/ppermute | solution.py:349
  219.6 45.0 %collective-permute-start.30 = (f32[16,2048]{1,0:T(8,128)S(1)}, f32[16,2048]{1,0:T(8,128)S(1)}, u32[]{:S(2)}, u32[]{:S(2)}) collective-permute-start(f32[16,2048]{1,0:T(8,128)S(1)} %add.78), channel_id=1, source_target_pairs={{0,8},{4,12},{8,0},{12,4},{16,24},{20,28},{24,16},{28,20},{1,9},{5... | collective-permute-start | bytes 393224 | tf_op jit(solution)/shard_map/ppermute | solution.py:258
  221.2 43.4 %collective-permute-start.31 = (bf16[128,2048]{1,0:T(8,128)(2,1)S(1)}, bf16[128,2048]{1,0:T(8,128)(2,1)S(1)}, u32[]{:S(2)}, u32[]{:S(2)}) collective-permute-start(bf16[128,2048]{1,0:T(8,128)(2,1)S(1)} %get-tuple-element.104), channel_id=1, source_target_pairs={{0,24},{4,28},{8,16},{12,20},{16,8},{20,12},{24,0},{28,4},{1,25},{... | collective-permute-start | bytes 1572872 | tf_op jit(solution)/shard_map/ppermute | solution.py:258
  225.3 39.3 %collective-permute-start.32 = (bf16[128,2048]{1,0:T(8,128)(2,1)}, bf16[128,2048]{1,0:T(8,128)(2,1)S(1)}, u32[]{:S(2)}, u32[]{:S(2)}) collective-permute-start(bf16[128,2048]{1,0:T(8,128)(2,1)} %get-tuple-element.118), channel_id=1, source_target_pairs={{0,8},{4,12},{8,0},{12,4},{16,24},{20,28},{24,16},{28,20},{1,9},{5... | collective-permute-start | bytes 1572872 | tf_op jit(solution)/shard_map/ppermute | solution.py:258
  226.9 37.7 %collective-permute-start.33 = (bf16[128,2048]{1,0:T(8,128)(2,1)}, bf16[128,2048]{1,0:T(8,128)(2,1)S(1)}, u32[]{:S(2)}, u32[]{:S(2)}) collective-permute-start(bf16[128,2048]{1,0:T(8,128)(2,1)} %get-tuple-element.117), channel_id=1, source_target_pairs={{0,16},{4,20},{8,24},{12,28},{16,0},{20,4},{24,8},{28,12},{1,17},{... | collective-permute-start | bytes 1572872 | tf_op jit(solution)/shard_map/ppermute | solution.py:258
  229.4 35.2 %collective-permute-start.34 = (bf16[128,2048]{1,0:T(8,128)(2,1)}, bf16[128,2048]{1,0:T(8,128)(2,1)S(1)}, u32[]{:S(2)}, u32[]{:S(2)}) collective-permute-start(bf16[128,2048]{1,0:T(8,128)(2,1)} %get-tuple-element.116), channel_id=1, source_target_pairs={{0,24},{4,28},{8,16},{12,20},{16,8},{20,12},{24,0},{28,4},{1,25},{... | collective-permute-start | bytes 1572872 | tf_op jit(solution)/shard_map/ppermute | solution.py:258
  (27 other events, 288.3 us)

commit v2 on v1

--- a/solution.py
+++ b/solution.py
@@ -66,7 +66,7 @@
         )
 
     gate_copy = part(wc, wc_s, 0, both)
-    up_copy = part(wc, wc_s, both, both + LANES)
+    up_copy = part(wc, wc_s, both, both + LANES + LANES * own)
     wd_copy = pltpu.make_async_copy(wd, wd_s, sems.at[next(taken)])
     acc_copies = []
     if not own:
@@ -90,7 +90,7 @@
 
     def chunk(c, carry):
         here = pl.ds(pl.multiple_of(c * chunk_rows, chunk_rows), chunk_rows)
-        pre_s[...] = mm(x_s[here, :width], wc_s[...], NN)
+        pre_s[...] = mm(x_s[here, :width], wc_s[:, : 2 * both + LANES], NN)
         score = jax.nn.sigmoid(pre_s[:, 2 * both :])
         chosen = score * x_s[here, width:].astype(F32)
         gates = chosen / jnp.sum(chosen, axis=1, keepdims=True)
@@ -174,8 +174,7 @@
 
         def token(c, carry):
             here = pl.ds(pl.multiple_of(c * chunk_rows, chunk_rows), chunk_rows)
-            grad = mm(gu[here, : 2 * both + LANES], wc_s[...], NT)
-            x_s[here, :width] = (grad + mm(gu[here, 2 * both + LANES :], wc_s[:, 2 * both :], NT)).astype(BF16)
+            x_s[here, :width] = mm(gu[here, :], wc_s[...], NT).astype(BF16)
             return carry
 
         finals = []
@@ -223,7 +222,7 @@
     scratch = [
         pltpu.VMEM((rows, width + LANES), BF16),
         pltpu.VMEM((rows, width), BF16),
-        pltpu.VMEM((width, 2 * both + LANES), BF16),
+        pltpu.VMEM((width, 2 * both + LANES + LANES * own), BF16),
         pltpu.VMEM((both, width), BF16),
         pltpu.VMEM((chunk, 2 * both + LANES), F32),
         pltpu.VMEM((rows, both), F32),
@@ -298,6 +297,9 @@
     def along(b):
         return lax.ppermute(b, "dp", ring)
 
+    def against(b):
+        return lax.ppermute(b, "dp", [(j, i) for i, j in ring])
+
     def hold(*values):
         return lax.optimization_barrier(values)
 
@@ -318,23 +320,24 @@
         return mine.astype(BF16)
 
     one = along(block)
+    two_x, two_o = against(block[:tok]), against(block[tok:])
     pair0 = pair_of(block)
     near0 = over_link(pair0)
     near0, one, wc = hold(near0, one, wc)
-    diag0, other0, two, pair1 = onward(near0), swap(near0), along(one), pair_of(one)
-    diag0, other0, one, pair1, two = hold(diag0, other0, one, pair1, two)
+    diag0, other0, pair1 = onward(near0), swap(near0), pair_of(one)
+    diag0, other0, one, pair1, two_x = hold(diag0, other0, one, pair1, two_x)
     blocks0 = [pair0, near0, other0, diag0, swap(diag0)]
 
     near1, diag1 = over_link(pair1), along(diag0)
-    three, sibling2 = along(two), swap(two)
+    three, sibling2 = along(one), swap(two_x)
     acc, mixed_low, mixed_high, token_low, token_high, rp = experts(0, None, blocks0)
-    acc, mixed_low, mixed_high, token_low, token_high, rp, near1, diag1, three, sibling2 = hold(
-        acc, mixed_low, mixed_high, token_low, token_high, rp, near1, diag1, three, sibling2
+    acc, mixed_low, mixed_high, token_low, token_high, rp, near1, diag1, two_o, three, sibling2 = hold(
+        acc, mixed_low, mixed_high, token_low, token_high, rp, near1, diag1, two_o, three, sibling2
     )
     blocks1 = [pair1, near1, swap(near1), diag1, swap(diag1)]
 
-    pair2 = jnp.concatenate([two, sibling2], axis=0)
-    near2, diag2 = over_link(pair2), along(diag1)
+    pair2 = jnp.concatenate([two_x, two_o, sibling2, swap(two_o)], axis=0)
+    near2, diag2 = over_link(pair2), against(diag0)
     pair3 = pair_of(three)
     rp = rp + swap(rp)
     rp_z = lax.ppermute(rp, "dp", [(i, i ^ 1) for i in range(n_dp)])
@@ -347,7 +350,7 @@
 
     rp = rp + rp_z
     rp_z = lax.ppermute(rp, "dp", [(i, i ^ 2) for i in range(n_dp)])
-    near3, diag3 = over_link(pair3), along(diag2)
+    near3, diag3 = over_link(pair3), along(diag1)
     mixed_sums = core_sums(mixed_low, mixed_other)
     mixed_x, mixed_y = flip(mixed_sums[1], 2, 2), flip(mixed_sums[2], 4, 4)
     (acc,) = experts(2, acc, blocks2)

time: 274 us -> 270 us (0.985)
  waiting for transfers between devices: 43.7 us -> 33 us
  starting transfers between devices: 33.2 us -> 37.5 us
    ppermute x6 -> x4, waiting for transfers between devices: 27.9 us -> 15.2 us  [along(): return lax.ppermute(b, 'dp', ring)]
    ppermute x0 -> x3, starting transfers between devices: none -> 10.8 us  [against(): return lax.ppermute(b, 'dp', [(j, i) for i, j in ring])]
    ppermute x0 -> x3, waiting for transfers between devices: none -> 10.3 us  [against(): return lax.ppermute(b, 'dp', [(j, i) for i, j in ring])]
    ppermute x28 -> x29, waiting for transfers between devices: 15.8 us -> 7.44 us  [flip(): lax.ppermute(x, 'expert', [(i, i ^ (odd if i % 2 else even)) for i in ran...]
    ppermute x6 -> x4, starting transfers between devices: 7.85 us -> 4.62 us  [along(): return lax.ppermute(b, 'dp', ring)]
    unnamed x38 -> x40, local copies, waits for them, and re-layouts: 15 us -> 16.4 us
    ppermute x28 -> x29, starting transfers between devices: 21.3 us -> 21.5 us  [flip(): lax.ppermute(x, 'expert', [(i, i ^ (odd if i % 2 else even)) for i in ran...]
  transfers between devices with their start and end apart: 36 -> 38, of which waited for: 8 -> 6; matrix products, arithmetic and copies ran while one was open for 10% -> 11% of each run, Pallas kernels for 58% -> 59%
where the time goes in v2:
time: 270 us; the launch traced here: 267 us
  Pallas kernels  157 us (58%)
  starting transfers between devices  37.5 us (14%)
  waiting for transfers between devices  33 us (12%)
  local copies, waits for them, and re-layouts  21.3 us (8%)
  other arithmetic  16.1 us (6%)
    pallas_call x4, Pallas kernels, expert_call(): pl.pallas_call(functools.partial(expert_kernel, own, last, tok, width, ff...  157 us
    ppermute x29, starting transfers between devices, flip(): lax.ppermute(x, 'expert', [(i, i ^ (odd if i % 2 else even)) for i in ran...  21.5 us
    unnamed x40, local copies, waits for them, and re-layouts  16.4 us
    ppermute x4, waiting for transfers between devices, along(): return lax.ppermute(b, 'dp', ring)  15.2 us
    ppermute x3, starting transfers between devices, against(): return lax.ppermute(b, 'dp', [(j, i) for i, j in ring])  10.8 us
    ppermute x3, waiting for transfers between devices, against(): return lax.ppermute(b, 'dp', [(j, i) for i, j in ring])  10.3 us
    ppermute x29, waiting for transfers between devices, flip(): lax.ppermute(x, 'expert', [(i, i ^ (odd if i % 2 else even)) for i in ran...  7.44 us
    convert_element_type x2, other arithmetic, core_sums(): (rows_of(low, j) + rows_of(other, j)).astype(BF16)  6.31 us
  transfers between devices with their start and end apart: 38, of which 6 were waited for; matrix products, arithmetic and copies ran while one was open for 11% of the time, Pallas kernels for 59%

profile of v2, /device:TPU:0, one launch (start us, length us, event | category | flops | bytes accessed | tf_op | source)
XLA Modules:
  0.0 266.5 jit_solution(2668949611830186077)
XLA Ops:
  2.9 2.3 pad_maximum_fusion.3
  5.6 2.6 collective-permute-start.2
  9.8 2.9 %collective-permute-start.1 = (bf16[512,2176]{1,0:T(8,128)(2,1)}, bf16[512,2176]{1,0:T(8,128)(2,1)}, u32[]{:S(2)}, u32[]{:S(2)}) collective-permute-start(bf16[512,2176]{1,0:T(8,128)(2,1)} %pad_maximum_fusion.refs_1_), channel_id=1, source_target_pairs={{0,8},{4,20},{8,0},{12,28},{16,24},{20,4},{24,16},{28,12},{1,9},{5... | collective-permute-start | bytes 6684680 | tf_op jit(solution)/shard_map/ppermute | solution.py:257
  12.6 1.8 bitcast_dynamic-update-slice_fusion.3
  14.4 1.8 bitcast_dynamic-update-slice_fusion.2
  18.2 3.5 %bitcast_dynamic-update-slice_fusion = bf16[2048,2816]{1,0:T(8,128)(2,1)} fusion(bf16[2048,2816]{1,0:T(8,128)(2,1)} %bitcast_dynamic-update-slice_fusion.1, bf16[2,2048,640]{2,1,0:T(8,128)(2,1)} %param.11), kind=kLoop, calls=%fused_computation | loop fusion | bytes 5242880
  23.7 12.0 %collective-permute-done.2 = bf16[256,2176]{1,0:T(8,128)(2,1)S(1)} collective-permute-done((bf16[256,2176]{1,0:T(8,128)(2,1)}, bf16[256,2176]{1,0:T(8,128)(2,1)S(1)}, u32[]{:S(2)}, u32[]{:S(2)}) %collective-permute-start.2) | collective-permute-done | bytes 1114144 | tf_op jit(solution)/shard_map/ppermute | solution.py:298
  35.6 2.7 %collective-permute-done.1.refs_2_ = bf16[512,2176]{1,0:T(8,128)(2,1)} collective-permute-done((bf16[512,2176]{1,0:T(8,128)(2,1)}, bf16[512,2176]{1,0:T(8,128)(2,1)}, u32[]{:S(2)}, u32[]{:S(2)}) %collective-permute-start.1) | collective-permute-done | bytes 2228256 | tf_op jit(solution)/shard_map/ppermute | solution.py:257
  40.2 2.1 collective-permute-start.3
  42.4 3.7 %collective-permute-start.6 = (bf16[128,2176]{1,0:T(8,128)(2,1)S(1)}, bf16[128,2176]{1,0:T(8,128)(2,1)S(1)}, u32[]{:S(2)}, u32[]{:S(2)}) collective-permute-start(bf16[128,2176]{1,0:T(8,128)(2,1)S(1)} %pad_maximum_fusion.4), channel_id=1, source_target_pairs={{1,0},{2,1},{3,2},{0,3},{5,4},{6,5},{7,6},{4,7},{9,8},{10,9},{11,1... | collective-permute-start | bytes 1671176 | tf_op jit(solution)/shard_map/ppermute | solution.py:301
  47.5 10.3 %collective-permute-done.6 = bf16[128,2176]{1,0:T(8,128)(2,1)S(1)} collective-permute-done((bf16[128,2176]{1,0:T(8,128)(2,1)S(1)}, bf16[128,2176]{1,0:T(8,128)(2,1)S(1)}, u32[]{:S(2)}, u32[]{:S(2)}) %collective-permute-start.6) | collective-permute-done | bytes 557088 | tf_op jit(solution)/shard_map/ppermute | solution.py:301
  58.5 4.3 %collective-permute-start.10 = (bf16[128,2176]{1,0:T(8,128)(2,1)S(1)}, bf16[128,2176]{1,0:T(8,128)(2,1)}, u32[]{:S(2)}, u32[]{:S(2)}) collective-permute-start(bf16[128,2176]{1,0:T(8,128)(2,1)S(1)} %concatenate.26), channel_id=1, source_target_pairs={{1,0},{2,1},{3,2},{0,3},{5,4},{6,5},{7,6},{4,7},{9,8},{10,9},{11,1... | collective-permute-start | bytes 1671176 | tf_op jit(solution)/shard_map/ppermute | solution.py:301
  64.4 55.9 %experts_own.1 = (f32[3,512,1280]{2,1,0:T(8,128)}, bf16[512,2048]{1,0:T(8,128)(2,1)}, bf16[512,2048]{1,0:T(8,128)(2,1)}, bf16[512,2048]{1,0:T(8,128)(2,1)}, bf16...) custom-call(s32[10]{0:T(128)} %stack.27.refs_0_, bf16[512,2176]{1,0:T(8,128)(2,1)} %pad_maximum_fusion.refs_1_, ...), custom_call_target="tpu_custom_call" | custom-call | flops 20132659200 | bytes 40000000 | tf_op jit(solution)/shard_map/experts_own/pallas_call | solution.py:238
  120.3 3.3 %collective-permute-done.11 = bf16[256,2176]{1,0:T(8,128)(2,1)S(1)} collective-permute-done((bf16[256,2176]{1,0:T(8,128)(2,1)}, bf16[256,2176]{1,0:T(8,128)(2,1)S(1)}, u32[]{:S(2)}, u32[]{:S(2)}) %collective-permute-start.11) | collective-permute-done | bytes 1114144 | tf_op jit(solution)/shard_map/ppermute | solution.py:298
  125.7 1.9 constant_dynamic-update-slice_fusion.2
  128.5 3.9 %collective-permute-done.19 = f32[16,2048]{1,0:T(8,128)S(1)} collective-permute-done((f32[16,2048]{1,0:T(8,128)}, f32[16,2048]{1,0:T(8,128)S(1)}, u32[]{:S(2)}, u32[]{:S(2)}) %collective-permute-start.19) | collective-permute-done | bytes 131104 | tf_op jit(solution)/shard_map/ppermute | solution.py:257
  135.4 2.9 %collective-permute-start.17 = (bf16[256,2176]{1,0:T(8,128)(2,1)}, bf16[256,2176]{1,0:T(8,128)(2,1)}, u32[]{:S(2)}, u32[]{:S(2)}) collective-permute-start(bf16[256,2176]{1,0:T(8,128)(2,1)} %collective-permute-done.3.refs_4_), channel_id=1, source_target_pairs={{1,0},{2,1},{3,2},{0,3},{5,4},{6,5},{7,6},{4,7},{9,8},{10,9},{11,1... | collective-permute-start | bytes 3342344 | tf_op jit(solution)/shard_map/ppermute | solution.py:301
  138.2 33.4 %experts_mid.2.refs_8_ = f32[3,512,1280]{2,1,0:T(8,128)} custom-call(s32[10]{0:T(128)} %stack.27.refs_0_, bf16[512,2176]{1,0:T(8,128)(2,1)} %copy-done.2, bf16[512,2176]{1,0:T(8,128)(2,1)} %collective-permute-done.8.refs_2_, bf16[512,2176]{1,0:T(8,128)(2,1)} %collective-permute-done.13.refs_3_, ...), custom_call_target="tpu_custom_call", output_to_operand_aliasing={{}: (8, {})} | custom-call | flops 20132659200 | bytes 40000000 | tf_op jit(solution)/shard_map/experts_mid/pallas_call | solution.py:238
  172.3 2.0 collective-permute-start.26
  175.9 3.0 %add_convert_fusion.5 = (bf16[128,2048]{1,0:T(8,128)(2,1)S(1)}, bf16[128,2048]{1,0:T(8,128)(2,1)}, bf16[128,2048]{1,0:T(8,128)(2,1)}) fusion(bf16[512,2048]{1,0:T(8,128)(2,1)} %collective-permute-done.21, bf16[512,2048]{1,0:T(8,128)(2,1)S(1)} %copy-done.4), kind=kLoop, calls=%fused_computation.13 | loop fusion | flops 3145728 | bytes 4718592 | tf_op jit(solution)/shard_map/convert_element_type | solution.py:314
  181.0 33.6 %experts_mid.3.refs_8_ = f32[3,512,1280]{2,1,0:T(8,128)} custom-call(s32[10]{0:T(128)} %stack.27.refs_0_, bf16[512,2176]{1,0:T(8,128)(2,1)} %constant_dynamic-update-slice_fusion.refs_1_, bf16[512,2176]{1,0:T(8,128)(2,1)} %collective-permute-done.16.refs_2_, bf16[512,2176]{1,0:T(8,128)(2,1)} %collective-permute-done.23.refs_3_, ...), custom_call_target="tpu_custom_call", output_to_operand_aliasing={{}: (8, {})} | custom-call | flops 20132659200 | bytes 40000000 | tf_op jit(solution)/shard_map/experts_mid/pallas_call | solution.py:238
  217.9 3.3 %add_convert_fusion.2 = (bf16[128,2048]{1,0:T(8,128)(2,1)}, bf16[128,2048]{1,0:T(8,128)(2,1)}, bf16[128,2048]{1,0:T(8,128)(2,1)}) fusion(bf16[512,2048]{1,0:T(8,128)(2,1)} %collective-permute-done.22, bf16[512,2048]{1,0:T(8,128)(2,1)} %get-tuple-element.109), kind=kLoop, calls=%fused_computation.10 | loop fusion | flops 3145728 | bytes 4718592 | tf_op jit(solution)/shard_map/convert_element_type | solution.py:314
  226.2 34.3 %experts_last.1 = (bf16[2,512,640]{2,1,0:T(8,128)(2,1)}, bf16[2,512,640]{2,1,0:T(8,128)(2,1)}, bf16[2,640,512]{2,1,0:T(8,128)(2,1)}) custom-call(s32[10]{0:T(128)} %stack.27.refs_0_, bf16[512,2176]{1,0:T(8,128)(2,1)} %copy-done.3, bf16[512,2176]{1,0:T(8,128)(2,1)} %collective-permute-done.25.refs_2_, bf16[512,2176]{1,0:T(8,128)(2,1)} %copy-done.9, ...), custom_call_target="tpu_custom_call" | custom-call | flops 20132659200 | bytes 40000000 | tf_op jit(solution)/shard_map/experts_last/pallas_call | solution.py:238
  261.5 3.3 %add_convert_fusion = (bf16[128,2048]{1,0:T(8,128)(2,1)}, bf16[128,2048]{1,0:T(8,128)(2,1)}) fusion(bf16[128,2048]{1,0:T(8,128)(2,1)S(1)} %collective-permute-done.36, bf16[128,2048]{1,0:T(8,128)(2,1)S(1)} %collective-permute-done.35, bf16[128,2048]{1,0:T(8,128)(2,1)S(1)} %collective-permute-done.34, bf16[512,2048]{1,0:T(8,128)(2,1)} %collective-permute-done.22, ...), kind=kLoop, calls=%fused_computation.8 | loop fusion | flops 5242880 | bytes 6291456 | tf_op jit(solution)/shard_map/convert_element_type | solution.py:320
  (117 shorter events, 34.5 us)
Async XLA Ops:
  5.6 30.0 %collective-permute-start.2 = (bf16[256,2176]{1,0:T(8,128)(2,1)}, bf16[256,2176]{1,0:T(8,128)(2,1)S(1)}, u32[]{:S(2)}, u32[]{:S(2)}) collective-permute-start(bf16[256,2176]{1,0:T(8,128)(2,1)} %pad_maximum_fusion.3), channel_id=1, source_target_pairs={{0,1},{1,2},{2,3},{3,0},{4,5},{5,6},{6,7},{7,4},{8,9},{9,10},{10,1... | collective-permute-start | bytes 3342344 | tf_op jit(solution)/shard_map/ppermute | solution.py:298
  9.8 28.6 %collective-permute-start.1 = (bf16[512,2176]{1,0:T(8,128)(2,1)}, bf16[512,2176]{1,0:T(8,128)(2,1)}, u32[]{:S(2)}, u32[]{:S(2)}) collective-permute-start(bf16[512,2176]{1,0:T(8,128)(2,1)} %pad_maximum_fusion.refs_1_), channel_id=1, source_target_pairs={{0,8},{4,20},{8,0},{12,28},{16,24},{20,4},{24,16},{28,12},{1,9},{5... | collective-permute-start | bytes 6684680 | tf_op jit(solution)/shard_map/ppermute | solution.py:257
  38.4 19.4 %collective-permute-start.4 = (bf16[512,2176]{1,0:T(8,128)(2,1)}, bf16[512,2176]{1,0:T(8,128)(2,1)S(1)}, u32[]{:S(2)}, u32[]{:S(2)}) collective-permute-start(bf16[512,2176]{1,0:T(8,128)(2,1)} %collective-permute-done.1.refs_2_), channel_id=1, source_target_pairs={{0,4},{4,0},{8,12},{12,8},{16,20},{20,16},{24,28},{28,24},{1,5},{5... | collective-permute-start | bytes 6684680 | tf_op jit(solution)/shard_map/ppermute | solution.py:257
  40.2 17.6 %collective-permute-start.3 = (bf16[256,2176]{1,0:T(8,128)(2,1)S(1)}, bf16[256,2176]{1,0:T(8,128)(2,1)}, u32[]{:S(2)}, u32[]{:S(2)}) collective-permute-start(bf16[256,2176]{1,0:T(8,128)(2,1)S(1)} %slice.67), channel_id=1, source_target_pairs={{0,16},{4,12},{8,24},{12,4},{16,0},{20,28},{24,8},{28,20},{1,17},{... | collective-permute-start | bytes 3342344 | tf_op jit(solution)/shard_map/ppermute | solution.py:257
  57.9 65.8 %collective-permute-start.8 = (bf16[512,2176]{1,0:T(8,128)(2,1)S(1)}, bf16[512,2176]{1,0:T(8,128)(2,1)}, u32[]{:S(2)}, u32[]{:S(2)}) collective-permute-start(bf16[512,2176]{1,0:T(8,128)(2,1)S(1)} %pad_maximum_fusion.1.refs_1_), channel_id=1, source_target_pairs={{0,8},{4,20},{8,0},{12,28},{16,24},{20,4},{24,16},{28,12},{1,9},{5... | collective-permute-start | bytes 6684680 | tf_op jit(solution)/shard_map/ppermute | solution.py:257
  58.5 61.9 %collective-permute-start.10 = (bf16[128,2176]{1,0:T(8,128)(2,1)S(1)}, bf16[128,2176]{1,0:T(8,128)(2,1)}, u32[]{:S(2)}, u32[]{:S(2)}) collective-permute-start(bf16[128,2176]{1,0:T(8,128)(2,1)S(1)} %concatenate.26), channel_id=1, source_target_pairs={{1,0},{2,1},{3,2},{0,3},{5,4},{6,5},{7,6},{4,7},{9,8},{10,9},{11,1... | collective-permute-start | bytes 1671176 | tf_op jit(solution)/shard_map/ppermute | solution.py:301
  63.4 56.9 %collective-permute-start.9 = (bf16[256,2176]{1,0:T(8,128)(2,1)}, bf16[256,2176]{1,0:T(8,128)(2,1)}, u32[]{:S(2)}, u32[]{:S(2)}) collective-permute-start(bf16[256,2176]{1,0:T(8,128)(2,1)} %collective-permute-done.3.refs_4_), channel_id=1, source_target_pairs={{0,1},{1,2},{2,3},{3,0},{4,5},{5,6},{6,7},{7,4},{8,9},{9,10},{10,1... | collective-permute-start | bytes 3342344 | tf_op jit(solution)/shard_map/ppermute | solution.py:298
  63.4 60.2 %collective-permute-start.11 = (bf16[256,2176]{1,0:T(8,128)(2,1)}, bf16[256,2176]{1,0:T(8,128)(2,1)S(1)}, u32[]{:S(2)}, u32[]{:S(2)}) collective-permute-start(bf16[256,2176]{1,0:T(8,128)(2,1)} %copy-done.5), channel_id=1, source_target_pairs={{0,1},{1,2},{2,3},{3,0},{4,5},{5,6},{6,7},{7,4},{8,9},{9,10},{10,1... | collective-permute-start | bytes 3342344 | tf_op jit(solution)/shard_map/ppermute | solution.py:298
  63.4 56.9 %collective-permute-start.12 = (bf16[128,2176]{1,0:T(8,128)(2,1)S(1)}, bf16[128,2176]{1,0:T(8,128)(2,1)S(1)}, u32[]{:S(2)}, u32[]{:S(2)}) collective-permute-start(bf16[128,2176]{1,0:T(8,128)(2,1)S(1)} %collective-permute-done.6), channel_id=1, source_target_pairs={{0,4},{4,0},{8,12},{12,8},{16,20},{20,16},{24,28},{28,24},{1,5},{5... | collective-permute-start | bytes 1671176 | tf_op jit(solution)/shard_map/ppermute | solution.py:257
  132.3 39.4 %collective-permute-start.21 = (bf16[512,2048]{1,0:T(8,128)(2,1)}, bf16[512,2048]{1,0:T(8,128)(2,1)}, u32[]{:S(2)}, u32[]{:S(2)}) collective-permute-start(bf16[512,2048]{1,0:T(8,128)(2,1)} %get-tuple-element.84), channel_id=1, source_target_pairs={{0,4},{4,0},{8,12},{12,8},{16,20},{20,16},{24,28},{28,24},{1,5},{5... | collective-permute-start | bytes 6291464 | tf_op jit(solution)/shard_map/ppermute | solution.py:257
  132.6 39.2 %collective-permute-start.22 = (bf16[512,2048]{1,0:T(8,128)(2,1)}, bf16[512,2048]{1,0:T(8,128)(2,1)}, u32[]{:S(2)}, u32[]{:S(2)}) collective-permute-start(bf16[512,2048]{1,0:T(8,128)(2,1)} %get-tuple-element.85), channel_id=1, source_target_pairs={{0,4},{4,0},{8,12},{12,8},{16,20},{20,16},{24,28},{28,24},{1,5},{5... | collective-permute-start | bytes 6291464 | tf_op jit(solution)/shard_map/ppermute | solution.py:257
  133.8 37.9 %collective-permute-start.16 = (bf16[512,2176]{1,0:T(8,128)(2,1)}, bf16[512,2176]{1,0:T(8,128)(2,1)}, u32[]{:S(2)}, u32[]{:S(2)}) collective-permute-start(bf16[512,2176]{1,0:T(8,128)(2,1)} %constant_dynamic-update-slice_fusion.refs_1_), channel_id=1, source_target_pairs={{0,8},{4,20},{8,0},{12,28},{16,24},{20,4},{24,16},{28,12},{1,9},{5... | collective-permute-start | bytes 6684680 | tf_op jit(solution)/shard_map/ppermute | solution.py:257
  135.4 36.3 %collective-permute-start.17 = (bf16[256,2176]{1,0:T(8,128)(2,1)}, bf16[256,2176]{1,0:T(8,128)(2,1)}, u32[]{:S(2)}, u32[]{:S(2)}) collective-permute-start(bf16[256,2176]{1,0:T(8,128)(2,1)} %collective-permute-done.3.refs_4_), channel_id=1, source_target_pairs={{1,0},{2,1},{3,2},{0,3},{5,4},{6,5},{7,6},{4,7},{9,8},{10,9},{11,1... | collective-permute-start | bytes 3342344 | tf_op jit(solution)/shard_map/ppermute | solution.py:301
  138.2 33.5 %collective-permute-start.20 = (f32[16,2048]{1,0:T(8,128)S(1)}, f32[16,2048]{1,0:T(8,128)S(1)}, u32[]{:S(2)}, u32[]{:S(2)}) collective-permute-start(f32[16,2048]{1,0:T(8,128)S(1)} %add.70), channel_id=1, source_target_pairs={{0,1},{1,0},{2,3},{3,2},{4,5},{5,4},{6,7},{7,6},{8,9},{9,8},{10,11... | collective-permute-start | bytes 393224 | tf_op jit(solution)/shard_map/ppermute | solution.py:343
  172.3 42.3 %collective-permute-start.26 = (bf16[256,2176]{1,0:T(8,128)(2,1)}, bf16[256,2176]{1,0:T(8,128)(2,1)}, u32[]{:S(2)}, u32[]{:S(2)}) collective-permute-start(bf16[256,2176]{1,0:T(8,128)(2,1)} %collective-permute-done.9.refs_4_), channel_id=1, source_target_pairs={{0,1},{1,2},{2,3},{3,0},{4,5},{5,6},{6,7},{7,4},{8,9},{9,10},{10,1... | collective-permute-start | bytes 3342344 | tf_op jit(solution)/shard_map/ppermute | solution.py:298
  174.4 40.3 %collective-permute-start.25 = (bf16[512,2176]{1,0:T(8,128)(2,1)S(1)}, bf16[512,2176]{1,0:T(8,128)(2,1)}, u32[]{:S(2)}, u32[]{:S(2)}) collective-permute-start(bf16[512,2176]{1,0:T(8,128)(2,1)S(1)} %pad_maximum_fusion.2.refs_1_), channel_id=1, source_target_pairs={{0,8},{4,20},{8,0},{12,28},{16,24},{20,4},{24,16},{28,12},{1,9},{5... | collective-permute-start | bytes 6684680 | tf_op jit(solution)/shard_map/ppermute | solution.py:257
  178.8 35.8 %collective-permute-start.27 = (bf16[128,2048]{1,0:T(8,128)(2,1)}, bf16[128,2048]{1,0:T(8,128)(2,1)S(1)}, u32[]{:S(2)}, u32[]{:S(2)}) collective-permute-start(bf16[128,2048]{1,0:T(8,128)(2,1)} %get-tuple-element.125), channel_id=1, source_target_pairs={{0,8},{4,12},{8,0},{12,4},{16,24},{20,28},{24,16},{28,20},{1,9},{5... | collective-permute-start | bytes 1572872 | tf_op jit(solution)/shard_map/ppermute | solution.py:257
  179.4 35.3 %collective-permute-start.28 = (bf16[128,2048]{1,0:T(8,128)(2,1)}, bf16[128,2048]{1,0:T(8,128)(2,1)S(1)}, u32[]{:S(2)}, u32[]{:S(2)}) collective-permute-start(bf16[128,2048]{1,0:T(8,128)(2,1)} %get-tuple-element.124), channel_id=1, source_target_pairs={{0,16},{4,20},{8,24},{12,28},{16,0},{20,4},{24,8},{28,12},{1,17},{... | collective-permute-start | bytes 1572872 | tf_op jit(solution)/shard_map/ppermute | solution.py:257
  180.4 34.3 %collective-permute-start.29 = (f32[16,2048]{1,0:T(8,128)S(1)}, f32[16,2048]{1,0:T(8,128)S(1)}, u32[]{:S(2)}, u32[]{:S(2)}) collective-permute-start(f32[16,2048]{1,0:T(8,128)S(1)} %add.74), channel_id=1, source_target_pairs={{0,2},{1,3},{2,0},{3,1},{4,6},{5,7},{6,4},{7,5},{8,10},{9,11},{10,... | collective-permute-start | bytes 393224 | tf_op jit(solution)/shard_map/ppermute | solution.py:352
  215.3 45.2 %collective-permute-start.32 = (f32[16,2048]{1,0:T(8,128)S(1)}, f32[16,2048]{1,0:T(8,128)S(1)}, u32[]{:S(2)}, u32[]{:S(2)}) collective-permute-start(f32[16,2048]{1,0:T(8,128)S(1)} %add.78), channel_id=1, source_target_pairs={{0,8},{4,12},{8,0},{12,4},{16,24},{20,28},{24,16},{28,20},{1,9},{5... | collective-permute-start | bytes 393224 | tf_op jit(solution)/shard_map/ppermute | solution.py:257
  216.5 44.0 %collective-permute-start.33 = (bf16[128,2048]{1,0:T(8,128)(2,1)S(1)}, bf16[128,2048]{1,0:T(8,128)(2,1)S(1)}, u32[]{:S(2)}, u32[]{:S(2)}) collective-permute-start(bf16[128,2048]{1,0:T(8,128)(2,1)S(1)} %get-tuple-element.108), channel_id=1, source_target_pairs={{0,24},{4,28},{8,16},{12,20},{16,8},{20,12},{24,0},{28,4},{1,25},{... | collective-permute-start | bytes 1572872 | tf_op jit(solution)/shard_map/ppermute | solution.py:257
  221.2 39.3 %collective-permute-start.34 = (bf16[128,2048]{1,0:T(8,128)(2,1)}, bf16[128,2048]{1,0:T(8,128)(2,1)S(1)}, u32[]{:S(2)}, u32[]{:S(2)}) collective-permute-start(bf16[128,2048]{1,0:T(8,128)(2,1)} %get-tuple-element.122), channel_id=1, source_target_pairs={{0,8},{4,12},{8,0},{12,4},{16,24},{20,28},{24,16},{28,20},{1,9},{5... | collective-permute-start | bytes 1572872 | tf_op jit(solution)/shard_map/ppermute | solution.py:257
  222.4 38.1 %collective-permute-start.35 = (bf16[128,2048]{1,0:T(8,128)(2,1)}, bf16[128,2048]{1,0:T(8,128)(2,1)S(1)}, u32[]{:S(2)}, u32[]{:S(2)}) collective-permute-start(bf16[128,2048]{1,0:T(8,128)(2,1)} %get-tuple-element.121), channel_id=1, source_target_pairs={{0,16},{4,20},{8,24},{12,28},{16,0},{20,4},{24,8},{28,12},{1,17},{... | collective-permute-start | bytes 1572872 | tf_op jit(solution)/shard_map/ppermute | solution.py:257
  224.7 35.8 %collective-permute-start.36 = (bf16[128,2048]{1,0:T(8,128)(2,1)}, bf16[128,2048]{1,0:T(8,128)(2,1)S(1)}, u32[]{:S(2)}, u32[]{:S(2)}) collective-permute-start(bf16[128,2048]{1,0:T(8,128)(2,1)} %get-tuple-element.120), channel_id=1, source_target_pairs={{0,24},{4,28},{8,16},{12,20},{16,8},{20,12},{24,0},{28,4},{1,25},{... | collective-permute-start | bytes 1572872 | tf_op jit(solution)/shard_map/ppermute | solution.py:257
  (29 other events, 339.7 us)
